TPU v7x, 32 devices: a whole 2x2x4 slice. The times are simulated.
32 devices in a mesh: region: 2 (over x), row: 4 (over z), col: 4 (over y, core).
Axes of the slice: x: 2, y: 2, z: 4, core: 2. Of those that a mesh axis runs over, the one named last changes fastest.
Arguments:
- covariance: float32 [8, 4096, 4096], P('region', 'row', 'col'), parts along dimension 0, as said below
- prior: float32 [16, 3, 256, 256], P('col'), may hold values from -0.21875 to 0.21875
- offsets: int32 [16, 3], replicated, may hold values from 0 to 15, as said below
- basis: float32 [8, 4096, 64], P('region', 'col'), parts along dimension 0, may hold values from -6 to 6
Outputs:
- whitened: float32 [8, 4096, 4096], P('region', 'row', 'col'), parts along dimension 0
- foreground_basis: float32 [8, 4096, 64], P('region', 'col'), parts along dimension 0
There are 2 independent parts, one for each index of `region`. A program takes and returns all parts, laid end to end along the dimension named above; an argument that names none is the same for every part. Nothing has to cross between parts.
Inputs may be any that keep to these rules, and one draw needn't show every extreme that they name: Row i of offsets begins with i; its other entries are distinct tile rows other than i, each within 2 of i. covariance is exactly symmetric in its last two dimensions.
All inputs are finite; a program needn't handle non-finite values.
Results may differ from a plain program's by a relative error of at most 0.0003.
Values sent between devices are 32-bit elements; how exact they have to be, the bound alone decides.
A program may use at most 320 MiB of HBM per device.

v0:
```python
import jax
import jax.numpy as jnp
from jax import lax
from jax.sharding import PartitionSpec as P

H = 2
ITERS = 2


full_precision = lax.Precision.HIGHEST


def with_halo(array, sides, width):
    for axis, dim in sides:
        peers, length = (lax.axis_size(axis), array.shape[dim])
        up = [(i, (i + 1) % peers) for i in range(peers - 1)]
        down = [(j, i) for i, j in up]
        last = lax.slice_in_dim(array, length - width, length, axis=dim)
        leading = lax.slice_in_dim(array, 0, width, axis=dim)
        before = lax.ppermute(last, axis, up)
        after = lax.ppermute(leading, axis, down)
        array = jnp.concatenate([before, array, after], axis=dim)
    return array


def from_behind(value, axis, steps):
    count = lax.axis_size(axis)
    leading, last = (max(0, -steps), min(count, count - steps))
    return lax.ppermute(value, axis, [(source, source + steps) for source in range(leading, last)])


def gram_matrix(modes):
    return jnp.einsum("snk,snl->skl", modes, modes, precision=full_precision)


def normalize(modes, gram):
    lower = jnp.linalg.cholesky(gram)
    return lax.linalg.triangular_solve(lower, modes, left_side=False, lower=True, transpose_a=True)


def band_blocks(source, offsets_row, start_shift, tile_size, axis_pos):
    picked = []
    for slot in range(offsets_row.shape[0]):
        picked.append(
            lax.dynamic_slice_in_dim(
                source, offsets_row[slot] * tile_size - start_shift, tile_size, axis_pos
            )
        )
    return jnp.stack(picked, axis=1)


def shards(covariance, prior, offsets, basis):
    scale_count, rows_dev, cols_dev = covariance.shape
    tile_size = prior.shape[2]
    row_tiles = rows_dev // tile_size
    col_tiles = cols_dev // tile_size
    row_pos = lax.axis_index("row")
    col_pos = lax.axis_index("col")
    band_reach = H * tile_size
    first_row = row_pos * row_tiles
    everything = lax.all_gather(prior, "col", axis=0, tiled=True)
    left_prior = lax.dynamic_slice_in_dim(everything, first_row, row_tiles, 0)
    padded = with_halo(covariance, (("row", 1),), band_reach)
    row_anchor = first_row * tile_size - band_reach
    left_tiles = []
    for local_tile in range(row_tiles):
        offsets_row = lax.dynamic_index_in_dim(offsets, first_row + local_tile, 0, keepdims=False)
        blocks = band_blocks(padded, offsets_row, row_anchor, tile_size, 1)
        left_tiles.append(
            jnp.einsum("bpq,sbqm->spm", left_prior[local_tile], blocks, precision=full_precision)
        )
    whitened_left = jnp.concatenate(left_tiles, axis=1)
    reach_steps = -(-band_reach // cols_dev)
    lower_side = []
    upper_side = []
    for step_no in range(1, reach_steps + 1):
        for direction in (step_no, -step_no):
            moved = from_behind(whitened_left, "col", direction)
            if direction > 0:
                lower_side.insert(0, moved)
            else:
                upper_side.append(moved)
    widened = jnp.concatenate(lower_side + [whitened_left] + upper_side, axis=2)
    col_anchor = (col_pos - reach_steps) * cols_dev
    first_col = col_pos * col_tiles
    right_tiles = []
    for local_tile in range(col_tiles):
        offsets_row = lax.dynamic_index_in_dim(offsets, first_col + local_tile, 0, keepdims=False)
        blocks = band_blocks(widened, offsets_row, col_anchor, tile_size, 2)
        right_tiles.append(
            jnp.einsum("sbmp,bqp->smq", blocks, prior[local_tile], precision=full_precision)
        )
    whitened = jnp.concatenate(right_tiles, axis=2)
    current = basis
    for sweep in range(ITERS):
        partial_modes = jnp.einsum("smn,snk->smk", whitened, current, precision=full_precision)
        modes = lax.psum(partial_modes, "col")
        gram = lax.psum(gram_matrix(modes), "row")
        gathered = lax.all_gather(normalize(modes, gram), "row", axis=1, tiled=True)
        current = lax.dynamic_slice_in_dim(gathered, col_pos * cols_dev, cols_dev, 1)
    return (whitened, current)


def solution(mesh):
    placed = (P("region", "row", "col"), P("col", None, None, None), P(), P("region", "col", None))
    return jax.shard_map(
        shards,
        mesh=mesh,
        in_specs=placed,
        out_specs=(P("region", "row", "col"), P("region", "col", None)),
        check_vma=False,
    )
```

profile of v0, /device:TPU:0, one launch (start us, length us, event | category | flops | bytes accessed | tf_op | source)
XLA Modules:
  0.0 1127.6 jit_solution(12660416469279299702)
XLA Ops:
  38.5 165.8 %collective-permute-done = f32[4,512,1024]{2,1,0:T(8,128)} collective-permute-done((f32[4,512,1024]{2,1,0:T(8,128)}, f32[4,512,1024]{2,1,0:T(8,128)}, u32[]{:S(2)}, u32[]{:S(2)}) %collective-permute-start) | collective-permute-done | bytes 8388640 | tf_op jit(solution)/shard_map/ppermute | solution.py:20
  232.9 34.8 %dynamic-slice_bitcast_fusion.23 = (f32[4,1,256,1024]{3,2,1,0:T(8,128)}, f32[4,1,256,1024]{3,2,1,0:T(8,128)}, f32[4,1,256,1024]{3,2,1,0:T(8,128)}, f32[4,1,256,1...) fusion(f32[4,2048,1024]{2,1,0:T(8,128)} %constant_dynamic-updat, ...), kind=kLoop, calls=%fused_computation.74 | loop fusion | bytes 100663344 | tf_op jit(solution)/shard_map/stack | solution.py:49
  267.7 15.7 %fusion.69 = f32[4,256,1024]{2,1,0:T(8,128)S(1)} fusion(f32[4,1,256,1024]{3,2,1,0:T(8,128)} %get-tuple-element.32, f32[4,1,256,1024]{3,2,1,0:T(8,128)} %get-tuple-element.33, f32[4,1,256,1024]{3,2,1,0:T(8,128)} %get-tuple-element.22, f32[16,3,256,256]{3,2,1,0:T(8,128)} %all-gather.4.cloned.1.call-done, s32[]{:T(128)S(6)} %select_n.105), kind=kOutput, calls=%fused_computation.82 | convolution fusion | flops 9669967872 | bytes 17563652 | tf_op jit(solution)/shard_map/bpq,sbqm->spm/dot_general | solution.py:70
  283.4 31.6 %fusion.66 = f32[4,256,1024]{2,1,0:T(8,128)S(1)} fusion(f32[4,1,256,1024]{3,2,1,0:T(8,128)S(1)} %copy-done.9, f32[4,1,256,1024]{3,2,1,0:T(8,128)S(1)} %copy-done.10, f32[4,1,256,1024]{3,2,1,0:T(8,128)S(1)} %copy-done.11, f32[16,3,256,256]{3,2,1,0:T(8,128)} %all-gather.4.cloned.1.call-done, s32[]{:T(128)S(6)} %add.193), kind=kOutput, calls=%fused_computation.81 | convolution fusion | flops 9669967872 | bytes 17563652 | tf_op jit(solution)/shard_map/bpq,sbqm->spm/dot_general | solution.py:70
  315.1 16.2 %fusion.63 = f32[4,256,1024]{2,1,0:T(8,128)S(1)} fusion(f32[4,1,256,1024]{3,2,1,0:T(8,128)S(1)} %copy-done.8, f32[4,1,256,1024]{3,2,1,0:T(8,128)} %get-tuple-element.27, f32[4,1,256,1024]{3,2,1,0:T(8,128)} %get-tuple-element.28, f32[16,3,256,256]{3,2,1,0:T(8,128)} %all-gather.4.cloned.1.call-done, s32[]{:T(128)S(6)} %add.194), kind=kOutput, calls=%fused_computation.80 | convolution fusion | flops 9669967872 | bytes 17563652 | tf_op jit(solution)/shard_map/bpq,sbqm->spm/dot_general | solution.py:70
  331.4 19.3 %fusion.60 = f32[4,256,1024]{2,1,0:T(8,128)S(1)} fusion(f32[4,1,256,1024]{3,2,1,0:T(8,128)S(1)} %copy-done.5, f32[4,1,256,1024]{3,2,1,0:T(8,128)S(1)} %copy-done.6, f32[4,1,256,1024]{3,2,1,0:T(8,128)S(1)} %copy-done.7, f32[16,3,256,256]{3,2,1,0:T(8,128)} %all-gather.4.cloned.1.call-done, s32[]{:T(128)S(6)} %add.195), kind=kOutput, calls=%fused_computation.79 | convolution fusion | flops 9669967872 | bytes 17563652 | tf_op jit(solution)/shard_map/bpq,sbqm->spm/dot_general | solution.py:70
  392.3 42.3 %pad_maximum_fusion = f32[4,1024,3072]{2,1,0:T(8,128)} fusion(f32[4,1024,1024]{2,1,0:T(8,128)} %collective-permute-done.3, f32[4,256,1024]{2,1,0:T(8,128)} %copy-done.4, f32[4,256,1024]{2,1,0:T(8,128)} %copy-done.3, f32[4,256,1024]{2,1,0:T(8,128)} %copy-done.2, f32[4,256,1024]{2,1,0:T(8,128)} %copy-done.1, f32[4,1024,1024]{2,1,0:T(8,128)} %collective-permute-done.2), kind=kLoop, calls=%fused_computation | loop fusion | flops 62914560 | bytes 100663296 | tf_op jit(solution)/shard_map/concatenate | solution.py:83
  434.7 32.1 %dynamic-slice_bitcast_fusion.11 = (f32[4,1,1024,256]{3,2,1,0:T(8,128)}, f32[4,1,1024,256]{3,2,1,0:T(8,128)S(1)}, f32[4,1,1024,256]{3,2,1,0:T(8,128)}, f32[4,1,1...) fusion(f32[4,1024,3072]{2,1,0:T(8,128)} %pad_maximum_fusion, ...), kind=kLoop, calls=%fused_computation.62 | loop fusion | bytes 100663344 | tf_op jit(solution)/shard_map/stack | solution.py:49
  466.8 15.9 %fusion.57 = f32[4,1024,256]{1,2,0:T(8,128)} fusion(f32[4,1,1024,256]{3,2,1,0:T(8,128)} %get-tuple-element.20, f32[4,1,1024,256]{3,2,1,0:T(8,128)} %get-tuple-element.21, f32[4,1,1024,256]{3,2,1,0:T(8,128)} %get-tuple-element.10, f32[4,3,256,256]{3,2,1,0:T(8,128)} %param.8), kind=kOutput, calls=%fused_computation.78 | convolution fusion | flops 9669967872 | bytes 17563648 | tf_op jit(solution)/shard_map/sbmp,bqp->smq/dot_general | solution.py:91
  482.7 14.3 %fusion.54 = f32[4,1024,256]{1,2,0:T(8,128)} fusion(f32[4,1,1024,256]{3,2,1,0:T(8,128)S(1)} %copy-done.17, f32[4,1,1024,256]{3,2,1,0:T(8,128)S(1)} %copy-done.18, f32[4,1,1024,256]{3,2,1,0:T(8,128)S(1)} %copy-done.19, f32[4,3,256,256]{3,2,1,0:T(8,128)} %param.8), kind=kOutput, calls=%fused_computation.77 | convolution fusion | flops 9669967872 | bytes 17563648 | tf_op jit(solution)/shard_map/sbmp,bqp->smq/dot_general | solution.py:91
  497.0 14.1 %fusion.51 = f32[4,1024,256]{1,2,0:T(8,128)} fusion(f32[4,1,1024,256]{3,2,1,0:T(8,128)S(1)} %copy-done.14, f32[4,1,1024,256]{3,2,1,0:T(8,128)S(1)} %copy-done.15, f32[4,1,1024,256]{3,2,1,0:T(8,128)S(1)} %copy-done.16, f32[4,3,256,256]{3,2,1,0:T(8,128)} %param.8), kind=kOutput, calls=%fused_computation.76 | convolution fusion | flops 9669967872 | bytes 17563648 | tf_op jit(solution)/shard_map/sbmp,bqp->smq/dot_general | solution.py:91
  525.1 15.2 %fusion.99 = f32[4,1024,64]{1,2,0:T(8,128)} fusion(f32[4,1024,64]{1,2,0:T(8,128)S(1)} %copy-done, f32[4,1024,256]{1,2,0:T(8,128)} %fusion.48, f32[4,1024,256]{1,2,0:T(8,128)} %fusion.51, f32[4,1024,256]{1,2,0:T(8,128)} %fusion.54, f32[4,1024,256]{1,2,0:T(8,128)} %fusion.57), kind=kOutput, calls=%fused_computation.138 | convolution fusion | flops 3233808384 | bytes 18874368 | tf_op jit(solution)/shard_map/smn,snk->smk/dot_general | solution.py:96
  540.4 191.0 %all-reduce.5.cloned.1.call-done = f32[4,1024,64]{1,2,0:T(8,128)} async-done(((f32[4,1024,64]{1,2,0:T(8,128)}), f32[4,1024,64]{1,2,0:T(8,128)}) %all-reduce.5.cloned.1.call-update) | async-done | bytes 1048592 | tf_op jit(solution)/shard_map/psum | solution.py:97
  734.8 35.2 %all-reduce.7.cloned.1.call-done = f32[4,64,64]{1,2,0:T(8,128)} async-done(((f32[4,64,64]{1,2,0:T(8,128)}), f32[4,64,64]{1,2,0:T(8,128)}) %all-reduce.7.cloned.1.call-update) | async-done | bytes 65552 | tf_op jit(solution)/shard_map/psum | solution.py:98
  772.0 23.7 %custom-call.8 = f32[4,64,64]{2,1,0:T(8,128)S(1)} custom-call(f32[4,64,64]{2,1,0:T(8,128)S(1)} %fusion.85), custom_call_target="Cholesky" | custom-call | tf_op jit(solution)/shard_map/jit(cholesky)/cholesky | solution.py:37
  795.9 19.7 %custom-call.9 = f32[4,1,64,64]{2,3,1,0:T(8,128)S(1)} custom-call(f32[4,1,64,64]{3,2,1,0:T(8,128)S(1)} %select_bitcast_fusion.1), custom_call_target="InvertDiagBlocksLowerTriangular" | custom-call | tf_op jit(solution)/shard_map/triangular_solve/custom-call.0 | solution.py:38
  818.9 80.5 %all-gather.6.cloned.1.call-done = f32[4,4096,64]{1,2,0:T(8,128)} async-done(((f32[4,1024,64]{1,2,0:T(8,128)}), f32[4,4096,64]{1,2,0:T(8,128)}) %all-gather.6.cloned.1.call-update) | async-done | bytes 4194320 | tf_op jit(solution)/shard_map/all_gather | solution.py:99
  899.4 15.4 %fusion.72 = f32[4,1024,64]{1,2,0:T(8,128)} fusion(f32[4,4096,64]{1,2,0:T(8,128)} %all-gather.6.cloned.1.call-done, s32[]{:T(128)S(6)} %select_n.137, f32[4,1024,256]{1,2,0:T(8,128)} %fusion.48, f32[4,1024,256]{1,2,0:T(8,128)} %fusion.51, f32[4,1024,256]{1,2,0:T(8,128)} %fusion.54, f32[4,1024,256]{1,2,0:T(8,128)} %fusion.57), kind=kOutput, calls=%fused_computation.85 | convolution fusion | flops 3233808384 | bytes 18874372 | tf_op jit(solution)/shard_map/smn,snk->smk/dot_general | solution.py:96
  914.9 34.9 %all-reduce.9.cloned.1.call-done = f32[4,1024,64]{1,2,0:T(8,128)} async-done(((f32[4,1024,64]{1,2,0:T(8,128)}), f32[4,1024,64]{1,2,0:T(8,128)}) %all-reduce.9.cloned.1.call-update) | async-done | bytes 1048592 | tf_op jit(solution)/shard_map/psum | solution.py:97
  953.2 35.2 %all-reduce.11.cloned.1.call-done = f32[4,64,64]{1,2,0:T(8,128)} async-done(((f32[4,64,64]{1,2,0:T(8,128)}), f32[4,64,64]{1,2,0:T(8,128)}) %all-reduce.11.cloned.1.call-update) | async-done | bytes 65552 | tf_op jit(solution)/shard_map/psum | solution.py:98
  990.4 23.7 %custom-call.10 = f32[4,64,64]{2,1,0:T(8,128)S(1)} custom-call(f32[4,64,64]{2,1,0:T(8,128)S(1)} %fusion.83), custom_call_target="Cholesky" | custom-call | tf_op jit(solution)/shard_map/jit(cholesky)/cholesky | solution.py:37
  1014.4 19.7 %custom-call.11 = f32[4,1,64,64]{2,3,1,0:T(8,128)S(1)} custom-call(f32[4,1,64,64]{3,2,1,0:T(8,128)S(1)} %select_bitcast_fusion), custom_call_target="InvertDiagBlocksLowerTriangular" | custom-call | tf_op jit(solution)/shard_map/triangular_solve/custom-call.0 | solution.py:38
  1049.4 16.4 %copy.30 = f32[4,1024,1024]{2,1,0:T(8,128)} copy(f32[4,1024,1024]{1,2,0:T(8,128)} %pad_maximum_fusion.2) | data formatting | bytes 33554432
  1065.8 52.1 %all-gather.8.cloned.1.call-done = f32[4,4096,64]{1,2,0:T(8,128)} async-done(((f32[4,1024,64]{1,2,0:T(8,128)}), f32[4,4096,64]{1,2,0:T(8,128)}) %all-gather.8.cloned.1.call-update) | async-done | bytes 4194320 | tf_op jit(solution)/shard_map/all_gather | solution.py:99
  (93 shorter events, 132.7 us)
Async XLA Ops:
  7.2 518.0 %copy-start = (f32[4,1024,64]{1,2,0:T(8,128)S(1)}, f32[4,1024,64]{1,2,0:T(8,128)}, u32[]{:S(2)}) copy-start(f32[4,1024,64]{1,2,0:T(8,128)} %param.10) | copy-start | bytes 3145732
  7.2 260.5 %all-gather.4.cloned.1.call-start = ((), (), s32[]{:S(2)}) async-start(), calls=%async_computation | async-start | bytes 15728640 | tf_op jit(solution)/shard_map/all_gather | solution.py:61
  7.9 21.9 %copy-start.20 = (s32[16,3]{0,1:T(4,128)S(1)}, s32[16,3]{0,1:T(4,128)}, u32[]{:S(2)}) copy-start(s32[16,3]{0,1:T(4,128)} %param.9) | copy-start | bytes 580
  7.9 723.5 %all-reduce.5.cloned.1.call-start = ((), (), s32[]{:S(2)}) async-start(), calls=%async_computation.1 | async-start | bytes 2097152 | tf_op jit(solution)/shard_map/psum | solution.py:97
  19.0 185.3 %collective-permute-start = (f32[4,512,1024]{2,1,0:T(8,128)}, f32[4,512,1024]{2,1,0:T(8,128)}, u32[]{:S(2)}, u32[]{:S(2)}) collective-permute-start(f32[4,512,1024]{2,1,0:T(8,128)} %get-tuple-element.35), channel_id=1, source_target_pairs={{0,4},{4,8},{8,12},{1,5},{5,9},{9,13},{2,6},{6,10},{10,14},{3,7},{... | collective-permute-start | bytes 25165832 | tf_op jit(solution)/shard_map/ppermute | solution.py:20
  28.5 196.0 %collective-permute-start.1 = (f32[4,512,1024]{2,1,0:T(8,128)}, f32[4,512,1024]{2,1,0:T(8,128)}, u32[]{:S(2)}, u32[]{:S(2)}) collective-permute-start(f32[4,512,1024]{2,1,0:T(8,128)} %get-tuple-element.34), channel_id=1, source_target_pairs={{4,0},{8,4},{12,8},{5,1},{9,5},{13,9},{6,2},{10,6},{14,10},{7,3},{... | collective-permute-start | bytes 25165832 | tf_op jit(solution)/shard_map/ppermute | solution.py:21
  267.7 15.7 %copy-start.9 = (f32[4,1,256,1024]{3,2,1,0:T(8,128)S(1)}, f32[4,1,256,1024]{3,2,1,0:T(8,128)}, u32[]{:S(2)}) copy-start(f32[4,1,256,1024]{3,2,1,0:T(8,128)} %get-tuple-element.29) | copy-start | bytes 12582916
  283.4 67.3 %copy-start.1 = (f32[4,256,1024]{2,1,0:T(8,128)}, f32[4,256,1024]{2,1,0:T(8,128)S(1)}, u32[]{:S(2)}) copy-start(f32[4,256,1024]{2,1,0:T(8,128)S(1)} %fusion.69) | copy-start | bytes 12582916
  283.4 31.7 %copy-start.8 = (f32[4,1,256,1024]{3,2,1,0:T(8,128)S(1)}, f32[4,1,256,1024]{3,2,1,0:T(8,128)}, u32[]{:S(2)}) copy-start(f32[4,1,256,1024]{3,2,1,0:T(8,128)} %get-tuple-element.26) | copy-start | bytes 12582916
  315.1 35.6 %copy-start.2 = (f32[4,256,1024]{2,1,0:T(8,128)}, f32[4,256,1024]{2,1,0:T(8,128)S(1)}, u32[]{:S(2)}) copy-start(f32[4,256,1024]{2,1,0:T(8,128)S(1)} %fusion.66) | copy-start | bytes 12582916
  315.1 16.2 %copy-start.5 = (f32[4,1,256,1024]{3,2,1,0:T(8,128)S(1)}, f32[4,1,256,1024]{3,2,1,0:T(8,128)}, u32[]{:S(2)}) copy-start(f32[4,1,256,1024]{3,2,1,0:T(8,128)} %get-tuple-element.23) | copy-start | bytes 12582916
  315.1 16.2 %copy-start.6 = (f32[4,1,256,1024]{3,2,1,0:T(8,128)S(1)}, f32[4,1,256,1024]{3,2,1,0:T(8,128)}, u32[]{:S(2)}) copy-start(f32[4,1,256,1024]{3,2,1,0:T(8,128)} %get-tuple-element.24) | copy-start | bytes 12582916
  315.1 16.2 %copy-start.7 = (f32[4,1,256,1024]{3,2,1,0:T(8,128)S(1)}, f32[4,1,256,1024]{3,2,1,0:T(8,128)}, u32[]{:S(2)}) copy-start(f32[4,1,256,1024]{3,2,1,0:T(8,128)} %get-tuple-element.25) | copy-start | bytes 12582916
  331.3 19.3 %copy-start.3 = (f32[4,256,1024]{2,1,0:T(8,128)}, f32[4,256,1024]{2,1,0:T(8,128)S(1)}, u32[]{:S(2)}) copy-start(f32[4,256,1024]{2,1,0:T(8,128)S(1)} %fusion.63) | copy-start | bytes 12582916
  357.9 26.4 %collective-permute-start.2 = (f32[4,1024,1024]{2,1,0:T(8,128)}, f32[4,1024,1024]{2,1,0:T(8,128)}, u32[]{:S(2)}, u32[]{:S(2)}) collective-permute-start(f32[4,1024,1024]{2,1,0:T(8,128)} %pad_maximum_fusion.1), channel_id=1, source_target_pairs={{0,1},{1,2},{2,3},{4,5},{5,6},{6,7},{8,9},{9,10},{10,11},{12,13},{... | collective-permute-start | bytes 50331656 | tf_op jit(solution)/shard_map/ppermute | solution.py:29
  364.9 27.4 %collective-permute-start.3 = (f32[4,1024,1024]{2,1,0:T(8,128)}, f32[4,1024,1024]{2,1,0:T(8,128)}, u32[]{:S(2)}, u32[]{:S(2)}) collective-permute-start(f32[4,1024,1024]{2,1,0:T(8,128)} %pad_maximum_fusion.1), channel_id=1, source_target_pairs={{1,0},{2,1},{3,2},{5,4},{6,5},{7,6},{9,8},{10,9},{11,10},{13,12},{... | collective-permute-start | bytes 50331656 | tf_op jit(solution)/shard_map/ppermute | solution.py:29
  466.7 15.9 %copy-start.17 = (f32[4,1,1024,256]{3,2,1,0:T(8,128)S(1)}, f32[4,1,1024,256]{3,2,1,0:T(8,128)}, u32[]{:S(2)}) copy-start(f32[4,1,1024,256]{3,2,1,0:T(8,128)} %get-tuple-element.17) | copy-start | bytes 12582916
  466.7 15.9 %copy-start.18 = (f32[4,1,1024,256]{3,2,1,0:T(8,128)S(1)}, f32[4,1,1024,256]{3,2,1,0:T(8,128)}, u32[]{:S(2)}) copy-start(f32[4,1,1024,256]{3,2,1,0:T(8,128)} %get-tuple-element.18) | copy-start | bytes 12582916
  466.8 15.9 %copy-start.19 = (f32[4,1,1024,256]{3,2,1,0:T(8,128)S(1)}, f32[4,1,1024,256]{3,2,1,0:T(8,128)}, u32[]{:S(2)}) copy-start(f32[4,1,1024,256]{3,2,1,0:T(8,128)} %get-tuple-element.19) | copy-start | bytes 12582916
  540.4 229.7 %all-reduce.7.cloned.1.call-start = ((), (), s32[]{:S(2)}) async-start(), calls=%async_computation.2 | async-start | bytes 262144 | tf_op jit(solution)/shard_map/psum | solution.py:98
  734.8 164.7 %all-gather.6.cloned.1.call-start = ((), (), s32[]{:S(2)}) async-start(), calls=%async_computation.3 | async-start | bytes 5242880 | tf_op jit(solution)/shard_map/all_gather | solution.py:99
  818.9 131.0 %all-reduce.9.cloned.1.call-start = ((), (), s32[]{:S(2)}) async-start(), calls=%async_computation.4 | async-start | bytes 2097152 | tf_op jit(solution)/shard_map/psum | solution.py:97
  914.9 73.6 %all-reduce.11.cloned.1.call-start = ((), (), s32[]{:S(2)}) async-start(), calls=%async_computation.5 | async-start | bytes 262144 | tf_op jit(solution)/shard_map/psum | solution.py:98
  953.2 164.7 %all-gather.8.cloned.1.call-start = ((), (), s32[]{:S(2)}) async-start(), calls=%async_computation.6 | async-start | bytes 5242880 | tf_op jit(solution)/shard_map/all_gather | solution.py:99
  (8 other events, 109.7 us)
Sparse Core Ops, SparseCore 0:
  9.5 84.7 all-gather.3
  540.5 190.8 all-reduce.4
  734.9 35.0 all-reduce.6
  819.0 80.4 all-gather.5
  915.0 34.7 all-reduce.8
  953.3 35.0 all-reduce.10
  1037.5 80.4 all-gather.7
where the time goes:
time: 1140 us; the launch traced here: 1130 us
  waiting for transfers between devices  613 us (54%)
  matrix products  185 us (16%)
  other arithmetic  151 us (13%)
  local copies, waits for them, and re-layouts  130 us (11%)
  between operations  30.1 us (3%)
  starting transfers between devices  19.4 us (2%)
    psum x2, waiting for transfers between devices, shards(): modes = lax.psum(partial_modes, 'col')  226 us
    ppermute x1, waiting for transfers between devices, with_halo(): before = lax.ppermute(last, axis, up)  166 us
    all_gather x2, waiting for transfers between devices, shards(): gathered = lax.all_gather(normalize(modes, gram), 'row', axis=1, tiled=True)  133 us
    dot_general x4, matrix products, shards(): jnp.einsum('bpq,sbqm->spm', left_prior[local_tile], blocks, precision=ful...  82.8 us
    psum x2, waiting for transfers between devices, shards(): gram = lax.psum(gram_matrix(modes), 'row')  70.4 us
    another operation x2, local copies, waits for them, and re-layouts, band_blocks(): return jnp.stack(picked, axis=1)  66.8 us
    dot_general x4, matrix products, shards(): jnp.einsum('sbmp,bqp->smq', blocks, prior[local_tile], precision=full_pre...  58.3 us
    another operation x7, other arithmetic, normalize(): lower = jnp.linalg.cholesky(gram)  47.8 us
  transfers between devices with their start and end apart: 11, of which 9 were waited for; matrix products, arithmetic and copies ran while one was open for 9% of the time, Pallas kernels for 0%

commit v1 on v0

v1 whole, which is shorter than its diff:
```python
import functools
import jax
import jax.numpy as jnp
from jax import lax
from jax.experimental import pallas as pl
from jax.experimental.pallas import tpu as pltpu
from jax.sharding import PartitionSpec as P

H = 2
ITERS = 2


full_precision = lax.Precision.HIGHEST
MESH = pl.DeviceIdType.MESH
NN = (((1,), (0,)), ((), ()))
NT = (((1,), (1,)), ((), ()))


def halos(array, axis, dim, width):
    peers, length = lax.axis_size(axis), array.shape[dim]
    before, after = [], []
    done, step = 0, 1
    while done < width:
        take = min(length, width - done)
        last = lax.slice_in_dim(array, length - take, length, axis=dim)
        lead = lax.slice_in_dim(array, 0, take, axis=dim)
        before.insert(0, lax.ppermute(last, axis, [(i, i + step) for i in range(peers - step)]))
        after.append(lax.ppermute(lead, axis, [(i + step, i) for i in range(peers - step)]))
        done, step = done + take, step + 1
    return before, after


def halves(x):
    high = x.astype(jnp.bfloat16)
    return high, (x - high.astype(jnp.float32)).astype(jnp.bfloat16)


def product(a, b, dims):
    ah, al = a
    bh, bl = b
    dot = functools.partial(lax.dot_general, dimension_numbers=dims, preferred_element_type=jnp.float32)
    return dot(ah, bh) + (dot(ah, bl) + dot(al, bh))


def left_kernel(slots, tab_ref, p_ref, *refs):
    out_ref = refs[-1]
    total = None
    for b in range(slots):
        term = product(halves(p_ref[0, b]), halves(refs[b][...]), NN)
        total = term if total is None else total + term
    out_ref[...] = total


def left_whiten(table, prior, padded, rows):
    tiles, slots, tile, _ = prior.shape
    cols = padded.shape[1]

    def band_map(b, i, tab):
        return (tab[i * slots + b], 0)

    return pl.pallas_call(
        functools.partial(left_kernel, slots),
        out_shape=jax.ShapeDtypeStruct((rows, cols), jnp.float32),
        grid_spec=pltpu.PrefetchScalarGridSpec(
            num_scalar_prefetch=1,
            grid=(tiles,),
            in_specs=[pl.BlockSpec((1, slots, tile, tile), lambda i, tab: (i, 0, 0, 0))]
            + [pl.BlockSpec((tile, cols), functools.partial(band_map, b)) for b in range(slots)],
            out_specs=pl.BlockSpec((tile, cols), lambda i, tab: (i, 0)),
        ),
        cost_estimate=pl.CostEstimate(
            flops=6 * rows * slots * tile * cols, bytes_accessed=4 * rows * cols * 4, transcendentals=0
        ),
        name="left_whiten",
    )(table, prior, *([padded] * slots))


def right_kernel(slots, aliased, tab_ref, p_ref, cur_ref, *refs):
    out_ref, modes_ref = refs[slots + aliased], refs[slots + aliased + 1]
    total = None
    for b in range(slots):
        term = product(halves(refs[b][...]), halves(p_ref[0, b]), NT)
        total = term if total is None else total + term
    out_ref[0] = total
    part = product(halves(cur_ref[...]), halves(total), NT)
    step = pl.program_id(0)

    @pl.when(step == 0)
    def _():
        modes_ref[...] = part

    @pl.when(step > 0)
    def _():
        modes_ref[...] += part


def right_whiten(table, prior, widened, current, scale, scales, cols, held):
    tiles, slots, tile, _ = prior.shape
    rows = widened.shape[0]
    modes = current.shape[0]

    def band_map(b, j, tab):
        return (0, tab[j * slots + b])

    aliased = 0 if held is None else 1
    in_specs = [
        pl.BlockSpec((1, slots, tile, tile), lambda j, tab: (j, 0, 0, 0)),
        pl.BlockSpec((modes, tile), lambda j, tab: (0, j)),
    ] + [pl.BlockSpec((rows, tile), functools.partial(band_map, b)) for b in range(slots)]
    args = [table, prior, current] + [widened] * slots
    aliases = {}
    if aliased:
        in_specs.append(pl.BlockSpec(memory_space=pl.ANY))
        aliases = {len(args): 0}
        args.append(held)
    return pl.pallas_call(
        functools.partial(right_kernel, slots, aliased),
        out_shape=(
            jax.ShapeDtypeStruct((scales, rows, cols), jnp.float32),
            jax.ShapeDtypeStruct((modes, rows), jnp.float32),
        ),
        grid_spec=pltpu.PrefetchScalarGridSpec(
            num_scalar_prefetch=1,
            grid=(tiles,),
            in_specs=in_specs,
            out_specs=[
                pl.BlockSpec((1, rows, tile), lambda j, tab: (scale, 0, j)),
                pl.BlockSpec((modes, rows), lambda j, tab: (0, 0)),
            ],
        ),
        input_output_aliases=aliases,
        cost_estimate=pl.CostEstimate(
            flops=6 * rows * slots * tile * cols, bytes_accessed=4 * rows * cols * 4, transcendentals=0
        ),
        name="right_whiten",
    )(*args)


def inverse_factor(gram):
    size = gram.shape[0]
    shape = (size, 2 * size)
    sub = lax.broadcasted_iota(jnp.int32, shape, 0)
    lane = lax.broadcasted_iota(jnp.int32, shape, 1)
    unit = jnp.where(lane == sub + size, 1.0, 0.0).astype(jnp.float32)
    start = jnp.concatenate([gram, unit[:, size:]], axis=1)

    def step(j, a):
        row = jnp.sum(jnp.where(sub == j, a, 0.0), axis=0, keepdims=True)
        col = jnp.sum(jnp.where(lane == j, a, 0.0), axis=1, keepdims=True)
        pivot = jnp.sum(jnp.where(lane[:1] == j, row, 0.0), axis=1, keepdims=True)
        scale = 1.0 / jnp.sqrt(pivot)
        row = row * scale
        return jnp.where(sub == j, row, jnp.where(sub > j, a - (col * scale) * row, a))

    return lax.fori_loop(0, size, step, start)[:, size:]


def reduce_kernel(axis, other, n, m, x_ref, out_ref, parts, grams, gath,
                  s_send, s_recv, g_send, g_recv, a_send, a_recv):
    me = lax.axis_index(axis)
    mine = lax.axis_index(other)
    chunk = x_ref.shape[0] // n

    barrier = pltpu.get_barrier_semaphore()
    for d in range(1, n):
        pl.semaphore_signal(barrier, inc=1, device_id={axis: lax.rem(me + d, n)}, device_id_type=MESH)
    for d in range(1, m):
        pl.semaphore_signal(barrier, inc=1, device_id={other: lax.rem(mine + d, m)}, device_id_type=MESH)
    pl.semaphore_wait(barrier, n + m - 2)

    scatter = []
    for d in range(1, n):
        peer = lax.rem(me + d, n)
        copy = pltpu.make_async_remote_copy(
            src_ref=x_ref.at[pl.ds(pl.multiple_of(peer * chunk, chunk), chunk), :],
            dst_ref=parts.at[d - 1],
            send_sem=s_send.at[d - 1],
            recv_sem=s_recv.at[d - 1],
            device_id={axis: peer},
            device_id_type=MESH,
        )
        copy.start()
        scatter.append(copy)
    modes = x_ref[pl.ds(pl.multiple_of(me * chunk, chunk), chunk), :]
    for d in range(1, n):
        scatter[d - 1].wait()
        modes = modes + parts[d - 1]

    grams[0] = lax.dot_general(
        modes, modes, NT, precision=full_precision, preferred_element_type=jnp.float32
    )
    sums = []
    for d in range(1, m):
        copy = pltpu.make_async_remote_copy(
            src_ref=grams.at[0],
            dst_ref=grams.at[d],
            send_sem=g_send.at[d - 1],
            recv_sem=g_recv.at[d - 1],
            device_id={other: lax.rem(mine + d, m)},
            device_id_type=MESH,
        )
        copy.start()
        sums.append(copy)
    gram = grams[0]
    for d in range(1, m):
        sums[d - 1].wait()
        gram = gram + grams[d]

    inverse = inverse_factor(gram)
    gath[0] = lax.dot_general(
        inverse, modes, NN, precision=full_precision, preferred_element_type=jnp.float32
    )
    gather = []
    for d in range(1, n):
        copy = pltpu.make_async_remote_copy(
            src_ref=gath.at[0],
            dst_ref=gath.at[d],
            send_sem=a_send.at[d - 1],
            recv_sem=a_recv.at[d - 1],
            device_id={axis: lax.rem(me + d, n)},
            device_id_type=MESH,
        )
        copy.start()
        gather.append(copy)
    out_ref[pl.ds(pl.multiple_of(me * chunk, chunk), chunk), :] = gath[0]
    for d in range(1, n):
        gather[d - 1].wait()
        owner = lax.rem(me + n - d, n)
        out_ref[pl.ds(pl.multiple_of(owner * chunk, chunk), chunk), :] = gath[d]


def reduce_normalize(partial, axis, other, number):
    scales, size, width = partial.shape
    n, m = lax.axis_size(axis), lax.axis_size(other)
    if n != scales:
        modes = lax.psum(partial, axis)
        gram = lax.psum(jnp.einsum("skm,slm->skl", modes, modes, precision=full_precision), other)
        lower = jnp.linalg.cholesky(gram)
        return lax.linalg.triangular_solve(lower, modes, left_side=True, lower=True)
    dma = pltpu.SemaphoreType.DMA
    flat = pl.pallas_call(
        functools.partial(reduce_kernel, axis, other, n, m),
        out_shape=jax.ShapeDtypeStruct((scales * size, width), jnp.float32),
        in_specs=[pl.BlockSpec(memory_space=pltpu.VMEM)],
        out_specs=pl.BlockSpec(memory_space=pltpu.VMEM),
        scratch_shapes=[
            pltpu.VMEM((n - 1, size, width), jnp.float32),
            pltpu.VMEM((m, size, size), jnp.float32),
            pltpu.VMEM((n, size, width), jnp.float32),
            dma((n - 1,)), dma((n - 1,)),
            dma((m - 1,)), dma((m - 1,)),
            dma((n - 1,)), dma((n - 1,)),
        ],
        compiler_params=pltpu.CompilerParams(collective_id=number, has_side_effects=True),
    )(partial.reshape(scales * size, width))
    return flat.reshape(scales, size, width)


def prior_of_rows(prior, row_tiles, first_row, row_pos, col_pos):
    rows, cols = lax.axis_size("row"), lax.axis_size("col")
    if rows == cols:
        total = jnp.where(row_pos == col_pos, prior, 0.0)
        for d in range(1, cols):
            pairs = [(r * cols + r, r * cols + (r + d) % cols) for r in range(rows)]
            moved = lax.ppermute(prior, ("row", "col"), pairs)
            total = jnp.where(col_pos == lax.rem(row_pos + d, cols), moved, total)
        return total
    everything = lax.all_gather(prior, "col", axis=0, tiled=True)
    return lax.dynamic_slice_in_dim(everything, first_row, row_tiles, 0)


def shards(covariance, prior, offsets, basis):
    scales, rows, cols = covariance.shape
    tile = prior.shape[2]
    reach = H * tile
    row_tiles, col_tiles = rows // tile, cols // tile
    row_pos, col_pos = lax.axis_index("row"), lax.axis_index("col")
    first_row, first_col = row_pos * row_tiles, col_pos * col_tiles

    slabs = []
    for s in range(scales):
        slabs.append(halos(covariance[s], "row", 0, reach))
    left_prior = prior_of_rows(prior, row_tiles, first_row, row_pos, col_pos)
    left_table = (lax.dynamic_slice_in_dim(offsets, first_row, row_tiles, 0) - first_row + H).reshape(-1)
    right_table = (lax.dynamic_slice_in_dim(offsets, first_col, col_tiles, 0) - first_col + H).reshape(-1)
    transposed = jnp.swapaxes(basis, 1, 2)

    whitened, parts = None, []
    for s in range(scales):
        before, after = slabs[s]
        if s:
            before, after, _ = lax.optimization_barrier((before, after, left))
        padded = jnp.concatenate(before + [covariance[s]] + after, axis=0)
        left = left_whiten(left_table, left_prior, padded, rows)
        before, after = halos(left, "col", 1, reach)
        widened = jnp.concatenate(before + [left] + after, axis=1)
        whitened, part = right_whiten(
            right_table, prior, widened, transposed[s], s, scales, cols, whitened
        )
        parts.append(part)

    current = reduce_normalize(jnp.stack(parts), "col", "row", 0)
    for sweep in range(1, ITERS):
        axis, other = ("row", "col") if sweep % 2 else ("col", "row")
        form = "skm,smn->skn" if sweep % 2 else "skn,smn->skm"
        partial = jnp.einsum(form, current, whitened, precision=lax.Precision.HIGH)
        current = reduce_normalize(partial, axis, other, sweep)
    return (whitened, jnp.swapaxes(current, 1, 2))


def solution(mesh):
    placed = (P("region", "row", "col"), P("col", None, None, None), P(), P("region", "col", None))
    return jax.shard_map(
        shards,
        mesh=mesh,
        in_specs=placed,
        out_specs=(P("region", "row", "col"), P("region", "col", None)),
        check_vma=False,
    )
```

time: 1140 us -> 456 us (0.40)
  waiting for transfers between devices: 613 us -> 73.3 us
  Pallas kernels: 0 us -> 209 us
  matrix products: 185 us -> 12.5 us
  other arithmetic: 151 us -> 48.8 us
  local copies, waits for them, and re-layouts: 130 us -> 44.6 us
  starting transfers between devices: 19.4 us -> 62.5 us
  between operations: 30.1 us -> 0.86 us
    psum x4 -> x0, waiting for transfers between devices: 296 us -> none  [the longest x2 226 us: shards(): modes = lax.psum(partial_modes, 'col')]
    pallas_call x0 -> x10, Pallas kernels: none -> 209 us  [the longest x2 107 us: reduce_normalize(): pl.pallas_call(functools.partial(reduce_kernel, axis, other, n, m), out_s...]
    dot_general x12 -> x1, matrix products: 178 us -> 12.5 us  [shards(): partial = jnp.einsum(form, current, whitened, precision=lax.Precision.HIGH)]
    all_gather x3 -> x0, waiting for transfers between devices: 133 us -> none  [the longest x2 133 us: shards(): gathered = lax.all_gather(normalize(modes, gram), 'row', axis=1, tiled=True)]
    ppermute x4 -> x19, waiting for transfers between devices: 183 us -> 73.3 us  [the longest x8 37.7 us: halos(): lax.ppermute(last, axis, [(i, i + step) for i in range(peers - step)])]
    another operation x12 -> x1, other arithmetic: 87.3 us -> 1.99 us  [shards(): current = reduce_normalize(jnp.stack(parts), 'col', 'row', 0)]
    another operation x2 -> x0, local copies, waits for them, and re-layouts: 66.8 us -> none  [band_blocks(): return jnp.stack(picked, axis=1)]
    ppermute x4 -> x19, starting transfers between devices: 19.1 us -> 62.5 us  [the longest x8 39.5 us: halos(): lax.ppermute(last, axis, [(i, i + step) for i in range(peers - step)])]
  transfers between devices with their start and end apart: 11 -> 19, of which waited for: 9 -> 5; matrix products, arithmetic and copies ran while one was open for 9% -> 18% of each run, Pallas kernels for 0% -> 20%
where the time goes in v1:
time: 456 us; the launch traced here: 452 us
  Pallas kernels  209 us (46%)
  waiting for transfers between devices  73.3 us (16%)
  starting transfers between devices  62.5 us (14%)
  other arithmetic  48.8 us (11%)
  local copies, waits for them, and re-layouts  44.6 us (10%)
  matrix products  12.5 us (3%)
    pallas_call x2, Pallas kernels, reduce_normalize(): pl.pallas_call(functools.partial(reduce_kernel, axis, other, n, m), out_s...  107 us
    pallas_call x4, Pallas kernels, right_whiten(): pl.pallas_call(functools.partial(right_kernel, slots, aliased), out_shape...  56.8 us
    pallas_call x4, Pallas kernels, left_whiten(): pl.pallas_call(functools.partial(left_kernel, slots), out_shape=jax.Shape...  46.1 us
    ppermute x8, starting transfers between devices, halos(): lax.ppermute(last, axis, [(i, i + step) for i in range(peers - step)])  39.5 us
    ppermute x8, waiting for transfers between devices, halos(): lax.ppermute(last, axis, [(i, i + step) for i in range(peers - step)])  37.7 us
    ppermute x8, waiting for transfers between devices, halos(): lax.ppermute(lead, axis, [(i + step, i) for i in range(peers - step)])  35.6 us
    slice x5, local copies, waits for them, and re-layouts, halos(): last = lax.slice_in_dim(array, length - take, length, axis=dim)  28.5 us
    concatenate x4, other arithmetic, shards(): padded = jnp.concatenate(before + [covariance[s]] + after, axis=0)  22.8 us
  transfers between devices with their start and end apart: 19, of which 5 were waited for; matrix products, arithmetic and copies ran while one was open for 18% of the time, Pallas kernels for 20%

profile of v1, /device:TPU:0, one launch (start us, length us, event | category | flops | bytes accessed | tf_op | source)
XLA Modules:
  0.0 452.0 jit_solution(14246147278474649613)
XLA Ops:
  9.7 12.2 %slice_bitcast_fusion.5 = (f32[512,1024]{1,0:T(8,128)}, f32[512,1024]{1,0:T(8,128)}, f32[512,1024]{1,0:T(8,128)}, f32[512,1024]{1,0:T(8,128)}, f32[512,1024]{1,0...) fusion(f32[4,1024,1024]{2,1,0:T(8,128)} %param.4), kind=kLoop, calls=%fused_computation.14 | loop fusion | bytes 33554432 | tf_op jit(solution)/shard_map/slice | solution.py:25
  29.7 37.7 %collective-permute-done.9 = f32[512,1024]{1,0:T(8,128)} collective-permute-done((f32[512,1024]{1,0:T(8,128)}, f32[512,1024]{1,0:T(8,128)}, u32[]{:S(2)}, u32[]{:S(2)}) %collective-permute-start.9) | collective-permute-done | bytes 2097184 | tf_op jit(solution)/shard_map/ppermute | solution.py:27
  76.3 11.3 %slice_bitcast_fusion = (f32[1024,1024]{1,0:T(8,128)}, f32[1024,1024]{1,0:T(8,128)}, f32[1024,1024]{1,0:T(8,128)S(1)}, f32[1024,1024]{1,0:T(8,128)}) fusion(f32[4,1024,1024]{2,1,0:T(8,128)} %param.4), kind=kLoop, calls=%fused_computation.8 | loop fusion | bytes 33554432 | tf_op jit(solution)/shard_map/squeeze | solution.py:282
  88.9 5.9 %collective-permute-start.5 = (f32[512,1024]{1,0:T(8,128)}, f32[512,1024]{1,0:T(8,128)}, u32[]{:S(2)}, u32[]{:S(2)}) collective-permute-start(f32[512,1024]{1,0:T(8,128)} %get-tuple-element.39), channel_id=1, source_target_pairs={{0,4},{4,8},{8,12},{1,5},{5,9},{9,13},{2,6},{6,10},{10,14},{3,7},{... | collective-permute-start | bytes 6291464 | tf_op jit(solution)/shard_map/ppermute | solution.py:27
  94.8 5.4 %pad_maximum_fusion.refs_0_.refs_1_.refs_2_ = f32[2048,1024]{1,0:T(8,128)} fusion(f32[512,1024]{1,0:T(8,128)} %collective-permute-done.10, f32[1024,1024]{1,0:T(8,128)S(1)} %get-tuple-element.32, f32[512,1024]{1,0:T(8,128)} %collective-permute-done.9), kind=kLoop, calls=%fused_computation | loop fusion | flops 4194304 | bytes 16777216 | tf_op jit(solution)/shard_map/concatenate | solution.py:293
  104.0 11.6 %left_whiten.4 = f32[1024,1024]{1,0:T(8,128)} custom-call(s32[12]{0:T(128)} %reshape.31.tab_ref, f32[4,3,256,256]{3,2,1,0:T(8,128)} %select_select_fusion.p_ref, f32[2048,1024]{1,0:T(8,128)} %pad_maximum_fusion.refs_0_.refs_1_.refs_2_, f32[2048,1024]{1,0:T(8,128)} %pad_maximum_fusion.refs_0_.refs_1_.refs_2_, f32[2048,1024]{1,0:T(8,128)} %pad_maximum_fusion.refs_0_.refs_1_.refs_2_), custom_call_target="tpu_custom_call" | custom-call | flops 4831838208 | bytes 16777216 | tf_op jit(solution)/shard_map/left_whiten/pallas_call | solution.py:61
  122.9 6.0 %pad_maximum_fusion.1.refs_0_.refs_1_.refs_2_ = f32[2048,1024]{1,0:T(8,128)} fusion(f32[512,1024]{1,0:T(8,128)} %collective-permute-done.8, f32[1024,1024]{1,0:T(8,128)} %get-tuple-element.31, f32[512,1024]{1,0:T(8,128)} %collective-permute-done.7), kind=kLoop, calls=%fused_computation.1 | loop fusion | flops 4194304 | bytes 16777216 | tf_op jit(solution)/shard_map/concatenate | solution.py:293
  129.0 11.5 %left_whiten.5 = f32[1024,1024]{1,0:T(8,128)} custom-call(s32[12]{0:T(128)} %reshape.31.tab_ref, f32[4,3,256,256]{3,2,1,0:T(8,128)} %select_select_fusion.p_ref, f32[2048,1024]{1,0:T(8,128)} %pad_maximum_fusion.1.refs_0_.refs_1_.refs_2_, f32[2048,1024]{1,0:T(8,128)} %pad_maximum_fusion.1.refs_0_.refs_1_.refs_2_, ...), custom_call_target="tpu_custom_call" | custom-call | flops 4831838208 | bytes 16777216 | tf_op jit(solution)/shard_map/left_whiten/pallas_call | solution.py:61
  140.4 23.1 %collective-permute-done.6 = f32[512,1024]{1,0:T(8,128)} collective-permute-done((f32[512,1024]{1,0:T(8,128)}, f32[512,1024]{1,0:T(8,128)}, u32[]{:S(2)}, u32[]{:S(2)}) %collective-permute-start.6) | collective-permute-done | bytes 2097184 | tf_op jit(solution)/shard_map/ppermute | solution.py:28
  163.6 6.0 %pad_maximum_fusion.2.refs_0_.refs_1_.refs_2_ = f32[2048,1024]{1,0:T(8,128)} fusion(f32[512,1024]{1,0:T(8,128)} %collective-permute-done.6, f32[1024,1024]{1,0:T(8,128)} %get-tuple-element.33, f32[512,1024]{1,0:T(8,128)} %collective-permute-done.5), kind=kLoop, calls=%fused_computation.2 | loop fusion | flops 4194304 | bytes 16777216 | tf_op jit(solution)/shard_map/concatenate | solution.py:293
  169.6 11.5 %left_whiten.6 = f32[1024,1024]{1,0:T(8,128)} custom-call(s32[12]{0:T(128)} %reshape.31.tab_ref, f32[4,3,256,256]{3,2,1,0:T(8,128)} %select_select_fusion.p_ref, f32[2048,1024]{1,0:T(8,128)} %pad_maximum_fusion.2.refs_0_.refs_1_.refs_2_, f32[2048,1024]{1,0:T(8,128)} %pad_maximum_fusion.2.refs_0_.refs_1_.refs_2_, ...), custom_call_target="tpu_custom_call" | custom-call | flops 4831838208 | bytes 16777216 | tf_op jit(solution)/shard_map/left_whiten/pallas_call | solution.py:61
  186.0 8.7 %collective-permute-start.13 = (f32[1024,512]{1,0:T(8,128)}, f32[1024,512]{1,0:T(8,128)}, u32[]{:S(2)}, u32[]{:S(2)}) collective-permute-start(f32[1024,512]{1,0:T(8,128)} %get-tuple-element.46), channel_id=1, source_target_pairs={{0,1},{1,2},{2,3},{4,5},{5,6},{6,7},{8,9},{9,10},{10,11},{12,13},{... | collective-permute-start | bytes 6291464 | tf_op jit(solution)/shard_map/ppermute | solution.py:27
  216.3 5.4 %collective-permute-start.17 = (f32[1024,512]{1,0:T(8,128)}, f32[1024,512]{1,0:T(8,128)}, u32[]{:S(2)}, u32[]{:S(2)}) collective-permute-start(f32[1024,512]{1,0:T(8,128)} %get-tuple-element.42), channel_id=1, source_target_pairs={{0,1},{1,2},{2,3},{4,5},{5,6},{6,7},{8,9},{9,10},{10,11},{12,13},{... | collective-permute-start | bytes 6291464 | tf_op jit(solution)/shard_map/ppermute | solution.py:27
  223.1 5.4 %pad_maximum_fusion.3.refs_0_.refs_1_.refs_2_ = f32[2048,1024]{1,0:T(8,128)} fusion(f32[512,1024]{1,0:T(8,128)} %collective-permute-done.4, f32[1024,1024]{1,0:T(8,128)S(1)} %copy-done.5, f32[512,1024]{1,0:T(8,128)} %collective-permute-done.3), kind=kLoop, calls=%fused_computation.3 | loop fusion | flops 4194304 | bytes 16777216 | tf_op jit(solution)/shard_map/concatenate | solution.py:293
  228.5 11.5 %left_whiten.7 = f32[1024,1024]{1,0:T(8,128)} custom-call(s32[12]{0:T(128)} %reshape.31.tab_ref, f32[4,3,256,256]{3,2,1,0:T(8,128)} %select_select_fusion.p_ref, f32[2048,1024]{1,0:T(8,128)} %pad_maximum_fusion.3.refs_0_.refs_1_.refs_2_, f32[2048,1024]{1,0:T(8,128)} %pad_maximum_fusion.3.refs_0_.refs_1_.refs_2_, ...), custom_call_target="tpu_custom_call" | custom-call | flops 4831838208 | bytes 16777216 | tf_op jit(solution)/shard_map/left_whiten/pallas_call | solution.py:61
  260.7 5.2 %pad_maximum_fusion.7.refs_0_.refs_1_.refs_2_ = f32[1024,2048]{1,0:T(8,128)} fusion(f32[1024,512]{1,0:T(8,128)} %collective-permute-done.18, f32[1024,1024]{1,0:T(8,128)S(1)} %copy-done.1, f32[1024,512]{1,0:T(8,128)} %collective-permute-done.17), kind=kLoop, calls=%fused_computation.7 | loop fusion | flops 4194304 | bytes 16777216 | tf_op jit(solution)/shard_map/concatenate | solution.py:296
  265.9 14.2 %right_whiten.4 = (f32[4,1024,1024]{2,1,0:T(8,128)}, f32[64,1024]{1,0:T(8,128)}) custom-call(s32[12]{0:T(128)} %reshape.30.tab_ref, f32[4,3,256,256]{3,2,1,0:T(8,128)} %p_ref.7, f32[64,1024]{1,0:T(8,128)} %get-tuple-element.50.cur_ref, f32[1024,2048]{1,0:T(8,128)} %pad_maximum_fusion.7.refs_0_.refs_1_.refs_2_, ...), custom_call_target="tpu_custom_call" | custom-call | flops 4831838208 | bytes 16777216 | tf_op jit(solution)/shard_map/right_whiten/pallas_call | solution.py:116
  280.1 14.2 %right_whiten.5 = (f32[4,1024,1024]{2,1,0:T(8,128)}, f32[64,1024]{1,0:T(8,128)}) custom-call(s32[12]{0:T(128)} %reshape.30.tab_ref, f32[4,3,256,256]{3,2,1,0:T(8,128)} %p_ref.7, f32[64,1024]{1,0:T(8,128)} %get-tuple-element.51.cur_ref, f32[1024,2048]{1,0:T(8,128)} %pad_maximum_fusion.6.refs_0_.refs_1_.refs_2_, ...), custom_call_target="tpu_custom_call", output_to_operand_aliasing={{0}: (6, {})} | custom-call | flops 4831838208 | bytes 16777216 | tf_op jit(solution)/shard_map/right_whiten/pallas_call | solution.py:116
  294.2 14.2 %right_whiten.6 = (f32[4,1024,1024]{2,1,0:T(8,128)}, f32[64,1024]{1,0:T(8,128)}) custom-call(s32[12]{0:T(128)} %reshape.30.tab_ref, f32[4,3,256,256]{3,2,1,0:T(8,128)} %p_ref.7, f32[64,1024]{1,0:T(8,128)} %get-tuple-element.52.cur_ref, f32[1024,2048]{1,0:T(8,128)} %pad_maximum_fusion.5.refs_0_.refs_1_.refs_2_, ...), custom_call_target="tpu_custom_call", output_to_operand_aliasing={{0}: (6, {})} | custom-call | flops 4831838208 | bytes 16777216 | tf_op jit(solution)/shard_map/right_whiten/pallas_call | solution.py:116
  308.4 5.9 %pad_maximum_fusion.4.refs_0_.refs_1_.refs_2_ = f32[1024,2048]{1,0:T(8,128)} fusion(f32[1024,512]{1,0:T(8,128)} %collective-permute-done.12, f32[1024,1024]{1,0:T(8,128)} %left_whiten.7, f32[1024,512]{1,0:T(8,128)} %collective-permute-done.11), kind=kLoop, calls=%fused_computation.4 | loop fusion | flops 4194304 | bytes 16777216 | tf_op jit(solution)/shard_map/concatenate | solution.py:296
  314.3 14.3 %right_whiten.7 = (f32[4,1024,1024]{2,1,0:T(8,128)}, f32[64,1024]{1,0:T(8,128)}) custom-call(s32[12]{0:T(128)} %reshape.30.tab_ref, f32[4,3,256,256]{3,2,1,0:T(8,128)} %p_ref.7, f32[64,1024]{1,0:T(8,128)} %get-tuple-element.53.cur_ref, f32[1024,2048]{1,0:T(8,128)} %pad_maximum_fusion.4.refs_0_.refs_1_.refs_2_, ...), custom_call_target="tpu_custom_call", output_to_operand_aliasing={{0}: (6, {})} | custom-call | flops 4831838208 | bytes 16777216 | tf_op jit(solution)/shard_map/right_whiten/pallas_call | solution.py:116
  330.6 46.0 %shard_map.59 = f32[256,1024]{1,0:T(8,128)} custom-call(f32[256,1024]{1,0:T(8,128)} %bitcast.47), custom_call_target="tpu_custom_call" | custom-call | tf_op jit(solution)/shard_map/pallas_call | solution.py:241
  376.7 12.5 %fusion.4 = f32[4,64,1024]{2,1,0:T(8,128)} fusion(f32[4,64,1024]{2,1,0:T(8,128)} %bitcast.45, f32[4,1024,1024]{2,1,0:T(8,128)} %get-tuple-element.58), kind=kOutput, calls=%fused_computation.32 | convolution fusion | flops 1610612736 | bytes 18874368 | tf_op jit(solution)/shard_map/skm,smn->skn/dot_general | solution.py:306
  389.1 60.5 %shard_map.60 = f32[256,1024]{1,0:T(8,128)} custom-call(f32[256,1024]{1,0:T(8,128)} %bitcast.46), custom_call_target="tpu_custom_call" | custom-call | tf_op jit(solution)/shard_map/pallas_call | solution.py:241
  (72 shorter events, 90.9 us)
Async XLA Ops:
  0.6 25.3 %copy-start = (f32[4,3,256,256]{3,2,1,0:T(8,128)S(1)}, f32[4,3,256,256]{3,2,1,0:T(8,128)}, u32[]{:S(2)}) copy-start(f32[4,3,256,256]{3,2,1,0:T(8,128)} %p_ref.7) | copy-start | bytes 9437188
  0.6 28.3 %copy-start.11 = (s32[16,3]{0,1:T(4,128)S(1)}, s32[16,3]{0,1:T(4,128)}, u32[]{:S(2)}) copy-start(s32[16,3]{0,1:T(4,128)} %param.6) | copy-start | bytes 580
  0.7 86.9 %collective-permute-start.2 = (f32[4,3,256,256]{3,2,1,0:T(8,128)}, f32[4,3,256,256]{3,2,1,0:T(8,128)}, u32[]{:S(2)}, u32[]{:S(2)}) collective-permute-start(f32[4,3,256,256]{3,2,1,0:T(8,128)} %p_ref.7), channel_id=1, source_target_pairs={{0,1},{5,6},{10,11},{15,12},{16,17},{21,22},{26,27},{31,28}} | collective-permute-start | bytes 9437192 | tf_op jit(solution)/shard_map/ppermute | solution.py:265
  5.0 83.9 %collective-permute-start.1 = (f32[4,3,256,256]{3,2,1,0:T(8,128)}, f32[4,3,256,256]{3,2,1,0:T(8,128)}, u32[]{:S(2)}, u32[]{:S(2)}) collective-permute-start(f32[4,3,256,256]{3,2,1,0:T(8,128)} %p_ref.7), channel_id=1, source_target_pairs={{0,2},{5,7},{10,8},{15,13},{16,18},{21,23},{26,24},{31,29}} | collective-permute-start | bytes 9437192 | tf_op jit(solution)/shard_map/ppermute | solution.py:265
  21.9 45.5 %collective-permute-start.9 = (f32[512,1024]{1,0:T(8,128)}, f32[512,1024]{1,0:T(8,128)}, u32[]{:S(2)}, u32[]{:S(2)}) collective-permute-start(f32[512,1024]{1,0:T(8,128)} %get-tuple-element.34), channel_id=1, source_target_pairs={{0,4},{4,8},{8,12},{1,5},{5,9},{9,13},{2,6},{6,10},{10,14},{3,7},{... | collective-permute-start | bytes 6291464 | tf_op jit(solution)/shard_map/ppermute | solution.py:27
  24.6 48.9 %collective-permute-start.10 = (f32[512,1024]{1,0:T(8,128)}, f32[512,1024]{1,0:T(8,128)}, u32[]{:S(2)}, u32[]{:S(2)}) collective-permute-start(f32[512,1024]{1,0:T(8,128)} %get-tuple-element.35), channel_id=1, source_target_pairs={{4,0},{8,4},{12,8},{5,1},{9,5},{13,9},{6,2},{10,6},{14,10},{7,3},{... | collective-permute-start | bytes 6291464 | tf_op jit(solution)/shard_map/ppermute | solution.py:28
  25.9 74.3 %collective-permute-start = (f32[4,3,256,256]{3,2,1,0:T(8,128)S(1)}, f32[4,3,256,256]{3,2,1,0:T(8,128)}, u32[]{:S(2)}, u32[]{:S(2)}) collective-permute-start(f32[4,3,256,256]{3,2,1,0:T(8,128)S(1)} %copy-done), channel_id=1, source_target_pairs={{0,3},{5,4},{10,9},{15,14},{16,19},{21,20},{26,25},{31,30}} | collective-permute-start | bytes 9437192 | tf_op jit(solution)/shard_map/ppermute | solution.py:265
  67.4 51.2 %collective-permute-start.8 = (f32[512,1024]{1,0:T(8,128)}, f32[512,1024]{1,0:T(8,128)}, u32[]{:S(2)}, u32[]{:S(2)}) collective-permute-start(f32[512,1024]{1,0:T(8,128)} %get-tuple-element.36), channel_id=1, source_target_pairs={{4,0},{8,4},{12,8},{5,1},{9,5},{13,9},{6,2},{10,6},{14,10},{7,3},{... | collective-permute-start | bytes 6291464 | tf_op jit(solution)/shard_map/ppermute | solution.py:28
  73.5 49.5 %collective-permute-start.7 = (f32[512,1024]{1,0:T(8,128)}, f32[512,1024]{1,0:T(8,128)}, u32[]{:S(2)}, u32[]{:S(2)}) collective-permute-start(f32[512,1024]{1,0:T(8,128)} %get-tuple-element.37), channel_id=1, source_target_pairs={{0,4},{4,8},{8,12},{1,5},{5,9},{9,13},{2,6},{6,10},{10,14},{3,7},{... | collective-permute-start | bytes 6291464 | tf_op jit(solution)/shard_map/ppermute | solution.py:27
  87.6 75.9 %collective-permute-start.6 = (f32[512,1024]{1,0:T(8,128)}, f32[512,1024]{1,0:T(8,128)}, u32[]{:S(2)}, u32[]{:S(2)}) collective-permute-start(f32[512,1024]{1,0:T(8,128)} %get-tuple-element.38), channel_id=1, source_target_pairs={{4,0},{8,4},{12,8},{5,1},{9,5},{13,9},{6,2},{10,6},{14,10},{7,3},{... | collective-permute-start | bytes 6291464 | tf_op jit(solution)/shard_map/ppermute | solution.py:28
  88.9 74.6 %collective-permute-start.5 = (f32[512,1024]{1,0:T(8,128)}, f32[512,1024]{1,0:T(8,128)}, u32[]{:S(2)}, u32[]{:S(2)}) collective-permute-start(f32[512,1024]{1,0:T(8,128)} %get-tuple-element.39), channel_id=1, source_target_pairs={{0,4},{4,8},{8,12},{1,5},{5,9},{9,13},{2,6},{6,10},{10,14},{3,7},{... | collective-permute-start | bytes 6291464 | tf_op jit(solution)/shard_map/ppermute | solution.py:27
  100.2 108.3 %collective-permute-start.4 = (f32[512,1024]{1,0:T(8,128)}, f32[512,1024]{1,0:T(8,128)}, u32[]{:S(2)}, u32[]{:S(2)}) collective-permute-start(f32[512,1024]{1,0:T(8,128)} %get-tuple-element.40), channel_id=1, source_target_pairs={{4,0},{8,4},{12,8},{5,1},{9,5},{13,9},{6,2},{10,6},{14,10},{7,3},{... | collective-permute-start | bytes 6291464 | tf_op jit(solution)/shard_map/ppermute | solution.py:28
  104.0 14.6 %copy-start.6 = (f32[512,1024]{1,0:T(8,128)S(1)}, f32[512,1024]{1,0:T(8,128)}, u32[]{:S(2)}) copy-start(f32[512,1024]{1,0:T(8,128)} %get-tuple-element.41) | copy-start | bytes 6291460
  118.6 92.9 %collective-permute-start.3 = (f32[512,1024]{1,0:T(8,128)S(1)}, f32[512,1024]{1,0:T(8,128)}, u32[]{:S(2)}, u32[]{:S(2)}) collective-permute-start(f32[512,1024]{1,0:T(8,128)S(1)} %copy-done.6), channel_id=1, source_target_pairs={{0,4},{4,8},{8,12},{1,5},{5,9},{9,13},{2,6},{6,10},{10,14},{3,7},{... | collective-permute-start | bytes 6291464 | tf_op jit(solution)/shard_map/ppermute | solution.py:27
  181.1 15.0 %copy-start.2 = (f32[1024,1024]{1,0:T(8,128)S(1)}, f32[1024,1024]{1,0:T(8,128)}, u32[]{:S(2)}) copy-start(f32[1024,1024]{1,0:T(8,128)} %left_whiten.5) | copy-start | bytes 12582916
  186.0 35.7 %collective-permute-start.13 = (f32[1024,512]{1,0:T(8,128)}, f32[1024,512]{1,0:T(8,128)}, u32[]{:S(2)}, u32[]{:S(2)}) collective-permute-start(f32[1024,512]{1,0:T(8,128)} %get-tuple-element.46), channel_id=1, source_target_pairs={{0,1},{1,2},{2,3},{4,5},{5,6},{6,7},{8,9},{9,10},{10,11},{12,13},{... | collective-permute-start | bytes 6291464 | tf_op jit(solution)/shard_map/ppermute | solution.py:27
  194.7 15.1 %copy-start.7 = (f32[4,1024,64]{1,2,0:T(8,128)S(1)}, f32[4,1024,64]{1,2,0:T(8,128)}, u32[]{:S(2)}) copy-start(f32[4,1024,64]{1,2,0:T(8,128)} %param.7) | copy-start | bytes 3145732
  194.7 49.4 %collective-permute-start.14 = (f32[1024,512]{1,0:T(8,128)}, f32[1024,512]{1,0:T(8,128)}, u32[]{:S(2)}, u32[]{:S(2)}) collective-permute-start(f32[1024,512]{1,0:T(8,128)} %get-tuple-element.47), channel_id=1, source_target_pairs={{1,0},{2,1},{3,2},{5,4},{6,5},{7,6},{9,8},{10,9},{11,10},{13,12},{... | collective-permute-start | bytes 6291464 | tf_op jit(solution)/shard_map/ppermute | solution.py:28
  198.7 55.2 %collective-permute-start.15 = (f32[1024,512]{1,0:T(8,128)}, f32[1024,512]{1,0:T(8,128)}, u32[]{:S(2)}, u32[]{:S(2)}) collective-permute-start(f32[1024,512]{1,0:T(8,128)} %get-tuple-element.44), channel_id=1, source_target_pairs={{0,1},{1,2},{2,3},{4,5},{5,6},{6,7},{8,9},{9,10},{10,11},{12,13},{... | collective-permute-start | bytes 6291464 | tf_op jit(solution)/shard_map/ppermute | solution.py:27
  208.5 47.0 %collective-permute-start.16 = (f32[1024,512]{1,0:T(8,128)}, f32[1024,512]{1,0:T(8,128)}, u32[]{:S(2)}, u32[]{:S(2)}) collective-permute-start(f32[1024,512]{1,0:T(8,128)} %get-tuple-element.45), channel_id=1, source_target_pairs={{1,0},{2,1},{3,2},{5,4},{6,5},{7,6},{9,8},{10,9},{11,10},{13,12},{... | collective-permute-start | bytes 6291464 | tf_op jit(solution)/shard_map/ppermute | solution.py:28
  216.3 44.4 %collective-permute-start.17 = (f32[1024,512]{1,0:T(8,128)}, f32[1024,512]{1,0:T(8,128)}, u32[]{:S(2)}, u32[]{:S(2)}) collective-permute-start(f32[1024,512]{1,0:T(8,128)} %get-tuple-element.42), channel_id=1, source_target_pairs={{0,1},{1,2},{2,3},{4,5},{5,6},{6,7},{8,9},{9,10},{10,11},{12,13},{... | collective-permute-start | bytes 6291464 | tf_op jit(solution)/shard_map/ppermute | solution.py:27
  221.6 39.0 %collective-permute-start.18 = (f32[1024,512]{1,0:T(8,128)}, f32[1024,512]{1,0:T(8,128)}, u32[]{:S(2)}, u32[]{:S(2)}) collective-permute-start(f32[1024,512]{1,0:T(8,128)} %get-tuple-element.43), channel_id=1, source_target_pairs={{1,0},{2,1},{3,2},{5,4},{6,5},{7,6},{9,8},{10,9},{11,10},{13,12},{... | collective-permute-start | bytes 6291464 | tf_op jit(solution)/shard_map/ppermute | solution.py:28
  244.2 64.3 %collective-permute-start.11 = (f32[1024,512]{1,0:T(8,128)}, f32[1024,512]{1,0:T(8,128)}, u32[]{:S(2)}, u32[]{:S(2)}) collective-permute-start(f32[1024,512]{1,0:T(8,128)} %get-tuple-element.48), channel_id=1, source_target_pairs={{0,1},{1,2},{2,3},{4,5},{5,6},{6,7},{8,9},{9,10},{10,11},{12,13},{... | collective-permute-start | bytes 6291464 | tf_op jit(solution)/shard_map/ppermute | solution.py:27
  253.9 54.5 %collective-permute-start.12 = (f32[1024,512]{1,0:T(8,128)S(1)}, f32[1024,512]{1,0:T(8,128)}, u32[]{:S(2)}, u32[]{:S(2)}) collective-permute-start(f32[1024,512]{1,0:T(8,128)S(1)} %get-tuple-element.49), channel_id=1, source_target_pairs={{1,0},{2,1},{3,2},{5,4},{6,5},{7,6},{9,8},{10,9},{11,10},{13,12},{... | collective-permute-start | bytes 6291464 | tf_op jit(solution)/shard_map/ppermute | solution.py:28
  (7 other events, 81.5 us)

commit v2 on v1

--- a/solution.py
+++ b/solution.py
@@ -36,19 +36,18 @@
 
 
 def product(a, b, dims):
-    ah, al = a
-    bh, bl = b
-    dot = functools.partial(lax.dot_general, dimension_numbers=dims, preferred_element_type=jnp.float32)
-    return dot(ah, bh) + (dot(ah, bl) + dot(al, bh))
+    (da,), (db,) = dims[0]
+    ah, al = zip(*map(halves, a))
+    bh, bl = zip(*map(halves, b))
+    left = jnp.concatenate(ah + ah + al, axis=da)
+    right = jnp.concatenate(bh + bl + bh, axis=db)
+    return lax.dot_general(left, right, dims, preferred_element_type=jnp.float32)
 
 
 def left_kernel(slots, tab_ref, p_ref, *refs):
     out_ref = refs[-1]
-    total = None
-    for b in range(slots):
-        term = product(halves(p_ref[0, b]), halves(refs[b][...]), NN)
-        total = term if total is None else total + term
-    out_ref[...] = total
+    band = range(slots)
+    out_ref[...] = product([p_ref[0, b] for b in band], [refs[b][...] for b in band], NN)
 
 
 def left_whiten(table, prior, padded, rows):
@@ -77,12 +76,10 @@
 
 def right_kernel(slots, aliased, tab_ref, p_ref, cur_ref, *refs):
     out_ref, modes_ref = refs[slots + aliased], refs[slots + aliased + 1]
-    total = None
-    for b in range(slots):
-        term = product(halves(refs[b][...]), halves(p_ref[0, b]), NT)
-        total = term if total is None else total + term
+    band = range(slots)
+    total = product([refs[b][...] for b in band], [p_ref[0, b] for b in band], NT)
     out_ref[0] = total
-    part = product(halves(cur_ref[...]), halves(total), NT)
+    part = product([cur_ref[...]], [total], NT)
     step = pl.program_id(0)
 
     @pl.when(step == 0)
@@ -145,14 +142,14 @@
     start = jnp.concatenate([gram, unit[:, size:]], axis=1)
 
     def step(j, a):
+        col = jnp.sum(jnp.where(lane == j, a, 0.0), axis=1, keepdims=True)
         row = jnp.sum(jnp.where(sub == j, a, 0.0), axis=0, keepdims=True)
-        col = jnp.sum(jnp.where(lane == j, a, 0.0), axis=1, keepdims=True)
-        pivot = jnp.sum(jnp.where(lane[:1] == j, row, 0.0), axis=1, keepdims=True)
-        scale = 1.0 / jnp.sqrt(pivot)
-        row = row * scale
-        return jnp.where(sub == j, row, jnp.where(sub > j, a - (col * scale) * row, a))
-
-    return lax.fori_loop(0, size, step, start)[:, size:]
+        pivot = jnp.sum(jnp.where(sub[:, :1] == j, col, 0.0), axis=0, keepdims=True)
+        return jnp.where(sub > j, a - (col * (1.0 / pivot)) * row, a)
+
+    a = lax.fori_loop(0, size, step, start)
+    pivots = jnp.sum(jnp.where(lane == sub, a, 0.0), axis=1, keepdims=True)
+    return (a / jnp.sqrt(pivots))[:, size:]
 
 
 def reduce_kernel(axis, other, n, m, x_ref, out_ref, parts, grams, gath,

time: 456 us -> 456 us (level)
  no operation moved by 1% of the time
where the time goes in v2:
time: 456 us; the launch traced here: 452 us
  Pallas kernels  209 us (46%)
  waiting for transfers between devices  73.3 us (16%)
  starting transfers between devices  62.5 us (14%)
  other arithmetic  48.8 us (11%)
  local copies, waits for them, and re-layouts  44.6 us (10%)
  matrix products  12.5 us (3%)
    pallas_call x2, Pallas kernels, reduce_normalize(): pl.pallas_call(functools.partial(reduce_kernel, axis, other, n, m), out_s...  106 us
    pallas_call x4, Pallas kernels, right_whiten(): pl.pallas_call(functools.partial(right_kernel, slots, aliased), out_shape...  57.1 us
    pallas_call x4, Pallas kernels, left_whiten(): pl.pallas_call(functools.partial(left_kernel, slots), out_shape=jax.Shape...  46.1 us
    ppermute x8, starting transfers between devices, halos(): lax.ppermute(last, axis, [(i, i + step) for i in range(peers - step)])  39.6 us
    ppermute x8, waiting for transfers between devices, halos(): lax.ppermute(last, axis, [(i, i + step) for i in range(peers - step)])  37.7 us
    ppermute x8, waiting for transfers between devices, halos(): lax.ppermute(lead, axis, [(i + step, i) for i in range(peers - step)])  35.6 us
    slice x5, local copies, waits for them, and re-layouts, halos(): last = lax.slice_in_dim(array, length - take, length, axis=dim)  28.5 us
    concatenate x4, other arithmetic, shards(): padded = jnp.concatenate(before + [covariance[s]] + after, axis=0)  22.8 us
  transfers between devices with their start and end apart: 19, of which 5 were waited for; matrix products, arithmetic and copies ran while one was open for 18% of the time, Pallas kernels for 20%

profile of v2, /device:TPU:0, one launch (start us, length us, event | category | flops | bytes accessed | tf_op | source)
XLA Modules:
  0.0 451.5 jit_solution(4535559451360531682)
XLA Ops:
  9.7 12.2 %slice_bitcast_fusion.5 = (f32[512,1024]{1,0:T(8,128)}, f32[512,1024]{1,0:T(8,128)}, f32[512,1024]{1,0:T(8,128)}, f32[512,1024]{1,0:T(8,128)}, f32[512,1024]{1,0...) fusion(f32[4,1024,1024]{2,1,0:T(8,128)} %param.4), kind=kLoop, calls=%fused_computation.14 | loop fusion | bytes 33554432 | tf_op jit(solution)/shard_map/slice | solution.py:25
  29.7 37.7 %collective-permute-done.9 = f32[512,1024]{1,0:T(8,128)} collective-permute-done((f32[512,1024]{1,0:T(8,128)}, f32[512,1024]{1,0:T(8,128)}, u32[]{:S(2)}, u32[]{:S(2)}) %collective-permute-start.9) | collective-permute-done | bytes 2097184 | tf_op jit(solution)/shard_map/ppermute | solution.py:27
  76.3 11.3 %slice_bitcast_fusion = (f32[1024,1024]{1,0:T(8,128)}, f32[1024,1024]{1,0:T(8,128)}, f32[1024,1024]{1,0:T(8,128)S(1)}, f32[1024,1024]{1,0:T(8,128)}) fusion(f32[4,1024,1024]{2,1,0:T(8,128)} %param.4), kind=kLoop, calls=%fused_computation.8 | loop fusion | bytes 33554432 | tf_op jit(solution)/shard_map/squeeze | solution.py:279
  88.9 5.9 %collective-permute-start.5 = (f32[512,1024]{1,0:T(8,128)}, f32[512,1024]{1,0:T(8,128)}, u32[]{:S(2)}, u32[]{:S(2)}) collective-permute-start(f32[512,1024]{1,0:T(8,128)} %get-tuple-element.39), channel_id=1, source_target_pairs={{0,4},{4,8},{8,12},{1,5},{5,9},{9,13},{2,6},{6,10},{10,14},{3,7},{... | collective-permute-start | bytes 6291464 | tf_op jit(solution)/shard_map/ppermute | solution.py:27
  94.8 5.4 %pad_maximum_fusion.refs_0_.refs_1_.refs_2_ = f32[2048,1024]{1,0:T(8,128)} fusion(f32[512,1024]{1,0:T(8,128)} %collective-permute-done.10, f32[1024,1024]{1,0:T(8,128)S(1)} %get-tuple-element.32, f32[512,1024]{1,0:T(8,128)} %collective-permute-done.9), kind=kLoop, calls=%fused_computation | loop fusion | flops 4194304 | bytes 16777216 | tf_op jit(solution)/shard_map/concatenate | solution.py:290
  104.0 11.6 %left_whiten.4 = f32[1024,1024]{1,0:T(8,128)} custom-call(s32[12]{0:T(128)} %reshape.31.tab_ref, f32[4,3,256,256]{3,2,1,0:T(8,128)} %select_select_fusion.p_ref, f32[2048,1024]{1,0:T(8,128)} %pad_maximum_fusion.refs_0_.refs_1_.refs_2_, f32[2048,1024]{1,0:T(8,128)} %pad_maximum_fusion.refs_0_.refs_1_.refs_2_, f32[2048,1024]{1,0:T(8,128)} %pad_maximum_fusion.refs_0_.refs_1_.refs_2_), custom_call_target="tpu_custom_call" | custom-call | flops 4831838208 | bytes 16777216 | tf_op jit(solution)/shard_map/left_whiten/pallas_call | solution.py:60
  122.9 6.0 %pad_maximum_fusion.1.refs_0_.refs_1_.refs_2_ = f32[2048,1024]{1,0:T(8,128)} fusion(f32[512,1024]{1,0:T(8,128)} %collective-permute-done.8, f32[1024,1024]{1,0:T(8,128)} %get-tuple-element.31, f32[512,1024]{1,0:T(8,128)} %collective-permute-done.7), kind=kLoop, calls=%fused_computation.1 | loop fusion | flops 4194304 | bytes 16777216 | tf_op jit(solution)/shard_map/concatenate | solution.py:290
  129.0 11.5 %left_whiten.5 = f32[1024,1024]{1,0:T(8,128)} custom-call(s32[12]{0:T(128)} %reshape.31.tab_ref, f32[4,3,256,256]{3,2,1,0:T(8,128)} %select_select_fusion.p_ref, f32[2048,1024]{1,0:T(8,128)} %pad_maximum_fusion.1.refs_0_.refs_1_.refs_2_, f32[2048,1024]{1,0:T(8,128)} %pad_maximum_fusion.1.refs_0_.refs_1_.refs_2_, ...), custom_call_target="tpu_custom_call" | custom-call | flops 4831838208 | bytes 16777216 | tf_op jit(solution)/shard_map/left_whiten/pallas_call | solution.py:60
  140.4 23.1 %collective-permute-done.6 = f32[512,1024]{1,0:T(8,128)} collective-permute-done((f32[512,1024]{1,0:T(8,128)}, f32[512,1024]{1,0:T(8,128)}, u32[]{:S(2)}, u32[]{:S(2)}) %collective-permute-start.6) | collective-permute-done | bytes 2097184 | tf_op jit(solution)/shard_map/ppermute | solution.py:28
  163.6 6.0 %pad_maximum_fusion.2.refs_0_.refs_1_.refs_2_ = f32[2048,1024]{1,0:T(8,128)} fusion(f32[512,1024]{1,0:T(8,128)} %collective-permute-done.6, f32[1024,1024]{1,0:T(8,128)} %get-tuple-element.33, f32[512,1024]{1,0:T(8,128)} %collective-permute-done.5), kind=kLoop, calls=%fused_computation.2 | loop fusion | flops 4194304 | bytes 16777216 | tf_op jit(solution)/shard_map/concatenate | solution.py:290
  169.6 11.5 %left_whiten.6 = f32[1024,1024]{1,0:T(8,128)} custom-call(s32[12]{0:T(128)} %reshape.31.tab_ref, f32[4,3,256,256]{3,2,1,0:T(8,128)} %select_select_fusion.p_ref, f32[2048,1024]{1,0:T(8,128)} %pad_maximum_fusion.2.refs_0_.refs_1_.refs_2_, f32[2048,1024]{1,0:T(8,128)} %pad_maximum_fusion.2.refs_0_.refs_1_.refs_2_, ...), custom_call_target="tpu_custom_call" | custom-call | flops 4831838208 | bytes 16777216 | tf_op jit(solution)/shard_map/left_whiten/pallas_call | solution.py:60
  186.0 8.7 %collective-permute-start.13 = (f32[1024,512]{1,0:T(8,128)}, f32[1024,512]{1,0:T(8,128)}, u32[]{:S(2)}, u32[]{:S(2)}) collective-permute-start(f32[1024,512]{1,0:T(8,128)} %get-tuple-element.46), channel_id=1, source_target_pairs={{0,1},{1,2},{2,3},{4,5},{5,6},{6,7},{8,9},{9,10},{10,11},{12,13},{... | collective-permute-start | bytes 6291464 | tf_op jit(solution)/shard_map/ppermute | solution.py:27
  216.3 5.4 %collective-permute-start.17 = (f32[1024,512]{1,0:T(8,128)}, f32[1024,512]{1,0:T(8,128)}, u32[]{:S(2)}, u32[]{:S(2)}) collective-permute-start(f32[1024,512]{1,0:T(8,128)} %get-tuple-element.42), channel_id=1, source_target_pairs={{0,1},{1,2},{2,3},{4,5},{5,6},{6,7},{8,9},{9,10},{10,11},{12,13},{... | collective-permute-start | bytes 6291464 | tf_op jit(solution)/shard_map/ppermute | solution.py:27
  223.1 5.4 %pad_maximum_fusion.3.refs_0_.refs_1_.refs_2_ = f32[2048,1024]{1,0:T(8,128)} fusion(f32[512,1024]{1,0:T(8,128)} %collective-permute-done.4, f32[1024,1024]{1,0:T(8,128)S(1)} %copy-done.5, f32[512,1024]{1,0:T(8,128)} %collective-permute-done.3), kind=kLoop, calls=%fused_computation.3 | loop fusion | flops 4194304 | bytes 16777216 | tf_op jit(solution)/shard_map/concatenate | solution.py:290
  228.5 11.5 %left_whiten.7 = f32[1024,1024]{1,0:T(8,128)} custom-call(s32[12]{0:T(128)} %reshape.31.tab_ref, f32[4,3,256,256]{3,2,1,0:T(8,128)} %select_select_fusion.p_ref, f32[2048,1024]{1,0:T(8,128)} %pad_maximum_fusion.3.refs_0_.refs_1_.refs_2_, f32[2048,1024]{1,0:T(8,128)} %pad_maximum_fusion.3.refs_0_.refs_1_.refs_2_, ...), custom_call_target="tpu_custom_call" | custom-call | flops 4831838208 | bytes 16777216 | tf_op jit(solution)/shard_map/left_whiten/pallas_call | solution.py:60
  260.7 5.2 %pad_maximum_fusion.7.refs_0_.refs_1_.refs_2_ = f32[1024,2048]{1,0:T(8,128)} fusion(f32[1024,512]{1,0:T(8,128)} %collective-permute-done.18, f32[1024,1024]{1,0:T(8,128)S(1)} %copy-done.1, f32[1024,512]{1,0:T(8,128)} %collective-permute-done.17), kind=kLoop, calls=%fused_computation.7 | loop fusion | flops 4194304 | bytes 16777216 | tf_op jit(solution)/shard_map/concatenate | solution.py:293
  265.9 14.2 %right_whiten.4 = (f32[4,1024,1024]{2,1,0:T(8,128)}, f32[64,1024]{1,0:T(8,128)}) custom-call(s32[12]{0:T(128)} %reshape.30.tab_ref, f32[4,3,256,256]{3,2,1,0:T(8,128)} %p_ref.7, f32[64,1024]{1,0:T(8,128)} %get-tuple-element.50.cur_ref, f32[1024,2048]{1,0:T(8,128)} %pad_maximum_fusion.7.refs_0_.refs_1_.refs_2_, ...), custom_call_target="tpu_custom_call" | custom-call | flops 4831838208 | bytes 16777216 | tf_op jit(solution)/shard_map/right_whiten/pallas_call | solution.py:113
  280.1 14.2 %right_whiten.5 = (f32[4,1024,1024]{2,1,0:T(8,128)}, f32[64,1024]{1,0:T(8,128)}) custom-call(s32[12]{0:T(128)} %reshape.30.tab_ref, f32[4,3,256,256]{3,2,1,0:T(8,128)} %p_ref.7, f32[64,1024]{1,0:T(8,128)} %get-tuple-element.51.cur_ref, f32[1024,2048]{1,0:T(8,128)} %pad_maximum_fusion.6.refs_0_.refs_1_.refs_2_, ...), custom_call_target="tpu_custom_call", output_to_operand_aliasing={{0}: (6, {})} | custom-call | flops 4831838208 | bytes 16777216 | tf_op jit(solution)/shard_map/right_whiten/pallas_call | solution.py:113
  294.4 14.2 %right_whiten.6 = (f32[4,1024,1024]{2,1,0:T(8,128)}, f32[64,1024]{1,0:T(8,128)}) custom-call(s32[12]{0:T(128)} %reshape.30.tab_ref, f32[4,3,256,256]{3,2,1,0:T(8,128)} %p_ref.7, f32[64,1024]{1,0:T(8,128)} %get-tuple-element.52.cur_ref, f32[1024,2048]{1,0:T(8,128)} %pad_maximum_fusion.5.refs_0_.refs_1_.refs_2_, ...), custom_call_target="tpu_custom_call", output_to_operand_aliasing={{0}: (6, {})} | custom-call | flops 4831838208 | bytes 16777216 | tf_op jit(solution)/shard_map/right_whiten/pallas_call | solution.py:113
  308.6 5.9 %pad_maximum_fusion.4.refs_0_.refs_1_.refs_2_ = f32[1024,2048]{1,0:T(8,128)} fusion(f32[1024,512]{1,0:T(8,128)} %collective-permute-done.12, f32[1024,1024]{1,0:T(8,128)} %left_whiten.7, f32[1024,512]{1,0:T(8,128)} %collective-permute-done.11), kind=kLoop, calls=%fused_computation.4 | loop fusion | flops 4194304 | bytes 16777216 | tf_op jit(solution)/shard_map/concatenate | solution.py:293
  314.5 14.4 %right_whiten.7 = (f32[4,1024,1024]{2,1,0:T(8,128)}, f32[64,1024]{1,0:T(8,128)}) custom-call(s32[12]{0:T(128)} %reshape.30.tab_ref, f32[4,3,256,256]{3,2,1,0:T(8,128)} %p_ref.7, f32[64,1024]{1,0:T(8,128)} %get-tuple-element.53.cur_ref, f32[1024,2048]{1,0:T(8,128)} %pad_maximum_fusion.4.refs_0_.refs_1_.refs_2_, ...), custom_call_target="tpu_custom_call", output_to_operand_aliasing={{0}: (6, {})} | custom-call | flops 4831838208 | bytes 16777216 | tf_op jit(solution)/shard_map/right_whiten/pallas_call | solution.py:113
  330.9 45.7 %shard_map.59 = f32[256,1024]{1,0:T(8,128)} custom-call(f32[256,1024]{1,0:T(8,128)} %bitcast.47), custom_call_target="tpu_custom_call" | custom-call | tf_op jit(solution)/shard_map/pallas_call | solution.py:238
  376.6 12.5 %fusion.4 = f32[4,64,1024]{2,1,0:T(8,128)} fusion(f32[4,64,1024]{2,1,0:T(8,128)} %bitcast.45, f32[4,1024,1024]{2,1,0:T(8,128)} %get-tuple-element.58), kind=kOutput, calls=%fused_computation.32 | convolution fusion | flops 1610612736 | bytes 18874368 | tf_op jit(solution)/shard_map/skm,smn->skn/dot_general | solution.py:303
  389.0 60.2 %shard_map.60 = f32[256,1024]{1,0:T(8,128)} custom-call(f32[256,1024]{1,0:T(8,128)} %bitcast.46), custom_call_target="tpu_custom_call" | custom-call | tf_op jit(solution)/shard_map/pallas_call | solution.py:238
  (72 shorter events, 90.9 us)
Async XLA Ops:
  0.6 25.3 %copy-start = (f32[4,3,256,256]{3,2,1,0:T(8,128)S(1)}, f32[4,3,256,256]{3,2,1,0:T(8,128)}, u32[]{:S(2)}) copy-start(f32[4,3,256,256]{3,2,1,0:T(8,128)} %p_ref.7) | copy-start | bytes 9437188
  0.6 28.3 %copy-start.11 = (s32[16,3]{0,1:T(4,128)S(1)}, s32[16,3]{0,1:T(4,128)}, u32[]{:S(2)}) copy-start(s32[16,3]{0,1:T(4,128)} %param.6) | copy-start | bytes 580
  0.7 86.9 %collective-permute-start.2 = (f32[4,3,256,256]{3,2,1,0:T(8,128)}, f32[4,3,256,256]{3,2,1,0:T(8,128)}, u32[]{:S(2)}, u32[]{:S(2)}) collective-permute-start(f32[4,3,256,256]{3,2,1,0:T(8,128)} %p_ref.7), channel_id=1, source_target_pairs={{0,1},{5,6},{10,11},{15,12},{16,17},{21,22},{26,27},{31,28}} | collective-permute-start | bytes 9437192 | tf_op jit(solution)/shard_map/ppermute | solution.py:262
  5.0 83.9 %collective-permute-start.1 = (f32[4,3,256,256]{3,2,1,0:T(8,128)}, f32[4,3,256,256]{3,2,1,0:T(8,128)}, u32[]{:S(2)}, u32[]{:S(2)}) collective-permute-start(f32[4,3,256,256]{3,2,1,0:T(8,128)} %p_ref.7), channel_id=1, source_target_pairs={{0,2},{5,7},{10,8},{15,13},{16,18},{21,23},{26,24},{31,29}} | collective-permute-start | bytes 9437192 | tf_op jit(solution)/shard_map/ppermute | solution.py:262
  21.9 45.5 %collective-permute-start.9 = (f32[512,1024]{1,0:T(8,128)}, f32[512,1024]{1,0:T(8,128)}, u32[]{:S(2)}, u32[]{:S(2)}) collective-permute-start(f32[512,1024]{1,0:T(8,128)} %get-tuple-element.34), channel_id=1, source_target_pairs={{0,4},{4,8},{8,12},{1,5},{5,9},{9,13},{2,6},{6,10},{10,14},{3,7},{... | collective-permute-start | bytes 6291464 | tf_op jit(solution)/shard_map/ppermute | solution.py:27
  24.6 48.9 %collective-permute-start.10 = (f32[512,1024]{1,0:T(8,128)}, f32[512,1024]{1,0:T(8,128)}, u32[]{:S(2)}, u32[]{:S(2)}) collective-permute-start(f32[512,1024]{1,0:T(8,128)} %get-tuple-element.35), channel_id=1, source_target_pairs={{4,0},{8,4},{12,8},{5,1},{9,5},{13,9},{6,2},{10,6},{14,10},{7,3},{... | collective-permute-start | bytes 6291464 | tf_op jit(solution)/shard_map/ppermute | solution.py:28
  25.9 74.3 %collective-permute-start = (f32[4,3,256,256]{3,2,1,0:T(8,128)S(1)}, f32[4,3,256,256]{3,2,1,0:T(8,128)}, u32[]{:S(2)}, u32[]{:S(2)}) collective-permute-start(f32[4,3,256,256]{3,2,1,0:T(8,128)S(1)} %copy-done), channel_id=1, source_target_pairs={{0,3},{5,4},{10,9},{15,14},{16,19},{21,20},{26,25},{31,30}} | collective-permute-start | bytes 9437192 | tf_op jit(solution)/shard_map/ppermute | solution.py:262
  67.4 51.2 %collective-permute-start.8 = (f32[512,1024]{1,0:T(8,128)}, f32[512,1024]{1,0:T(8,128)}, u32[]{:S(2)}, u32[]{:S(2)}) collective-permute-start(f32[512,1024]{1,0:T(8,128)} %get-tuple-element.36), channel_id=1, source_target_pairs={{4,0},{8,4},{12,8},{5,1},{9,5},{13,9},{6,2},{10,6},{14,10},{7,3},{... | collective-permute-start | bytes 6291464 | tf_op jit(solution)/shard_map/ppermute | solution.py:28
  73.5 49.5 %collective-permute-start.7 = (f32[512,1024]{1,0:T(8,128)}, f32[512,1024]{1,0:T(8,128)}, u32[]{:S(2)}, u32[]{:S(2)}) collective-permute-start(f32[512,1024]{1,0:T(8,128)} %get-tuple-element.37), channel_id=1, source_target_pairs={{0,4},{4,8},{8,12},{1,5},{5,9},{9,13},{2,6},{6,10},{10,14},{3,7},{... | collective-permute-start | bytes 6291464 | tf_op jit(solution)/shard_map/ppermute | solution.py:27
  87.6 75.9 %collective-permute-start.6 = (f32[512,1024]{1,0:T(8,128)}, f32[512,1024]{1,0:T(8,128)}, u32[]{:S(2)}, u32[]{:S(2)}) collective-permute-start(f32[512,1024]{1,0:T(8,128)} %get-tuple-element.38), channel_id=1, source_target_pairs={{4,0},{8,4},{12,8},{5,1},{9,5},{13,9},{6,2},{10,6},{14,10},{7,3},{... | collective-permute-start | bytes 6291464 | tf_op jit(solution)/shard_map/ppermute | solution.py:28
  88.9 74.6 %collective-permute-start.5 = (f32[512,1024]{1,0:T(8,128)}, f32[512,1024]{1,0:T(8,128)}, u32[]{:S(2)}, u32[]{:S(2)}) collective-permute-start(f32[512,1024]{1,0:T(8,128)} %get-tuple-element.39), channel_id=1, source_target_pairs={{0,4},{4,8},{8,12},{1,5},{5,9},{9,13},{2,6},{6,10},{10,14},{3,7},{... | collective-permute-start | bytes 6291464 | tf_op jit(solution)/shard_map/ppermute | solution.py:27
  100.2 108.3 %collective-permute-start.4 = (f32[512,1024]{1,0:T(8,128)}, f32[512,1024]{1,0:T(8,128)}, u32[]{:S(2)}, u32[]{:S(2)}) collective-permute-start(f32[512,1024]{1,0:T(8,128)} %get-tuple-element.40), channel_id=1, source_target_pairs={{4,0},{8,4},{12,8},{5,1},{9,5},{13,9},{6,2},{10,6},{14,10},{7,3},{... | collective-permute-start | bytes 6291464 | tf_op jit(solution)/shard_map/ppermute | solution.py:28
  104.0 14.6 %copy-start.6 = (f32[512,1024]{1,0:T(8,128)S(1)}, f32[512,1024]{1,0:T(8,128)}, u32[]{:S(2)}) copy-start(f32[512,1024]{1,0:T(8,128)} %get-tuple-element.41) | copy-start | bytes 6291460
  118.6 92.9 %collective-permute-start.3 = (f32[512,1024]{1,0:T(8,128)S(1)}, f32[512,1024]{1,0:T(8,128)}, u32[]{:S(2)}, u32[]{:S(2)}) collective-permute-start(f32[512,1024]{1,0:T(8,128)S(1)} %copy-done.6), channel_id=1, source_target_pairs={{0,4},{4,8},{8,12},{1,5},{5,9},{9,13},{2,6},{6,10},{10,14},{3,7},{... | collective-permute-start | bytes 6291464 | tf_op jit(solution)/shard_map/ppermute | solution.py:27
  181.1 15.0 %copy-start.2 = (f32[1024,1024]{1,0:T(8,128)S(1)}, f32[1024,1024]{1,0:T(8,128)}, u32[]{:S(2)}) copy-start(f32[1024,1024]{1,0:T(8,128)} %left_whiten.5) | copy-start | bytes 12582916
  186.0 35.7 %collective-permute-start.13 = (f32[1024,512]{1,0:T(8,128)}, f32[1024,512]{1,0:T(8,128)}, u32[]{:S(2)}, u32[]{:S(2)}) collective-permute-start(f32[1024,512]{1,0:T(8,128)} %get-tuple-element.46), channel_id=1, source_target_pairs={{0,1},{1,2},{2,3},{4,5},{5,6},{6,7},{8,9},{9,10},{10,11},{12,13},{... | collective-permute-start | bytes 6291464 | tf_op jit(solution)/shard_map/ppermute | solution.py:27
  194.7 15.1 %copy-start.7 = (f32[4,1024,64]{1,2,0:T(8,128)S(1)}, f32[4,1024,64]{1,2,0:T(8,128)}, u32[]{:S(2)}) copy-start(f32[4,1024,64]{1,2,0:T(8,128)} %param.7) | copy-start | bytes 3145732
  194.7 49.4 %collective-permute-start.14 = (f32[1024,512]{1,0:T(8,128)}, f32[1024,512]{1,0:T(8,128)}, u32[]{:S(2)}, u32[]{:S(2)}) collective-permute-start(f32[1024,512]{1,0:T(8,128)} %get-tuple-element.47), channel_id=1, source_target_pairs={{1,0},{2,1},{3,2},{5,4},{6,5},{7,6},{9,8},{10,9},{11,10},{13,12},{... | collective-permute-start | bytes 6291464 | tf_op jit(solution)/shard_map/ppermute | solution.py:28
  198.7 55.2 %collective-permute-start.15 = (f32[1024,512]{1,0:T(8,128)}, f32[1024,512]{1,0:T(8,128)}, u32[]{:S(2)}, u32[]{:S(2)}) collective-permute-start(f32[1024,512]{1,0:T(8,128)} %get-tuple-element.44), channel_id=1, source_target_pairs={{0,1},{1,2},{2,3},{4,5},{5,6},{6,7},{8,9},{9,10},{10,11},{12,13},{... | collective-permute-start | bytes 6291464 | tf_op jit(solution)/shard_map/ppermute | solution.py:27
  208.5 47.0 %collective-permute-start.16 = (f32[1024,512]{1,0:T(8,128)}, f32[1024,512]{1,0:T(8,128)}, u32[]{:S(2)}, u32[]{:S(2)}) collective-permute-start(f32[1024,512]{1,0:T(8,128)} %get-tuple-element.45), channel_id=1, source_target_pairs={{1,0},{2,1},{3,2},{5,4},{6,5},{7,6},{9,8},{10,9},{11,10},{13,12},{... | collective-permute-start | bytes 6291464 | tf_op jit(solution)/shard_map/ppermute | solution.py:28
  216.3 44.4 %collective-permute-start.17 = (f32[1024,512]{1,0:T(8,128)}, f32[1024,512]{1,0:T(8,128)}, u32[]{:S(2)}, u32[]{:S(2)}) collective-permute-start(f32[1024,512]{1,0:T(8,128)} %get-tuple-element.42), channel_id=1, source_target_pairs={{0,1},{1,2},{2,3},{4,5},{5,6},{6,7},{8,9},{9,10},{10,11},{12,13},{... | collective-permute-start | bytes 6291464 | tf_op jit(solution)/shard_map/ppermute | solution.py:27
  221.6 39.0 %collective-permute-start.18 = (f32[1024,512]{1,0:T(8,128)}, f32[1024,512]{1,0:T(8,128)}, u32[]{:S(2)}, u32[]{:S(2)}) collective-permute-start(f32[1024,512]{1,0:T(8,128)} %get-tuple-element.43), channel_id=1, source_target_pairs={{1,0},{2,1},{3,2},{5,4},{6,5},{7,6},{9,8},{10,9},{11,10},{13,12},{... | collective-permute-start | bytes 6291464 | tf_op jit(solution)/shard_map/ppermute | solution.py:28
  244.2 64.4 %collective-permute-start.11 = (f32[1024,512]{1,0:T(8,128)}, f32[1024,512]{1,0:T(8,128)}, u32[]{:S(2)}, u32[]{:S(2)}) collective-permute-start(f32[1024,512]{1,0:T(8,128)} %get-tuple-element.48), channel_id=1, source_target_pairs={{0,1},{1,2},{2,3},{4,5},{5,6},{6,7},{8,9},{9,10},{10,11},{12,13},{... | collective-permute-start | bytes 6291464 | tf_op jit(solution)/shard_map/ppermute | solution.py:27
  253.9 54.6 %collective-permute-start.12 = (f32[1024,512]{1,0:T(8,128)S(1)}, f32[1024,512]{1,0:T(8,128)}, u32[]{:S(2)}, u32[]{:S(2)}) collective-permute-start(f32[1024,512]{1,0:T(8,128)S(1)} %get-tuple-element.49), channel_id=1, source_target_pairs={{1,0},{2,1},{3,2},{5,4},{6,5},{7,6},{9,8},{10,9},{11,10},{13,12},{... | collective-permute-start | bytes 6291464 | tf_op jit(solution)/shard_map/ppermute | solution.py:28
  (7 other events, 81.7 us)
